TPU v7x, 256 devices: a whole 4x4x8 slice. The times are simulated.
256 devices in a mesh: depth: 4 (over y), cols: 64 (over z, x, core).
Axes of the slice: x: 4, y: 4, z: 8, core: 2. Of those that a mesh axis runs over, the one named last changes fastest.
Arguments:
- bricks: bfloat16 [4, 256, 256, 512], P('depth', 'cols'), may hold values from -6 to 6
- brick_owner: int32 [4, 65536, 1], P('depth', 'cols'), may hold values from 0 to 63; in each aligned block of 1024 rows (0 to 1023, 1024 to 2047, ..., all dimensions but the last counted through in order) at most 32 rows name the same one
- brick_slot: int32 [4, 65536], P('depth', 'cols'), may hold values from 0 to 3
- sample_base: int32 [4, 16, 65536], P('depth', None, 'cols'), may hold values from 0 to 3374
- corner_weights: bfloat16 [4, 8, 16, 65536], P('depth', None, None, 'cols'), may hold values from 0 to 1
- spacing: bfloat16 [4, 16, 65536], P('depth', None, 'cols'), may hold values from 0.029907227 to 0.079589844
- w_in: bfloat16 [128, 32], replicated, may hold values from -1 to 1
- w_mid: bfloat16 [128, 128], replicated, may hold values from -0.5 to 0.5
- w_last: bfloat16 [128, 128], replicated, may hold values from -0.5 to 0.5
- w_feat: bfloat16 [128, 128], replicated, may hold values from -0.5 to 0.5
- w_density: bfloat16 [1, 128], replicated, may hold values from -0.5 to 0.5
Outputs:
- image: float32 [128, 65536], P('depth', 'cols')
- visibility: float32 [4, 65536], P('depth', 'cols')
Inputs may be any that keep to these rules, and one draw needn't show every extreme that they name: `brick_owner`: within each region, among the 1024 rays of one index of cols, at most 32 name the same owner, a bound that some block reaches of them. `sample_base`: the cell i * 15**2 + j * 15 + k with i, j, k below 15.
All inputs are finite; a program needn't handle non-finite values.
Results may differ from a plain program's by a relative error of at most 0.0019.
Values may be sent and summed in bfloat16 or wider, within the bound.
A program may use at most 128 MiB of HBM per device.

v0:
```python
import jax
import jax.numpy as jnp
from jax import lax
from jax.sharding import PartitionSpec as P

EDGE = 16


def shifted(value, axis, steps):
    count = lax.axis_size(axis)
    initial, last = (max(0, -steps), min(count, count - steps))
    return lax.ppermute(value, axis, [(source, source + steps) for source in range(initial, last)])


def interpolate(flat_voxels, brick_index, base_cell, weights, edge_cells):
    cell_side = edge_cells - 1
    coord_x = base_cell // (cell_side * cell_side)
    coord_y = base_cell // cell_side % cell_side
    coord_z = base_cell % cell_side
    samples, extent = base_cell.shape
    channels = flat_voxels.shape[1]
    total = jnp.zeros((samples, extent, channels), jnp.float32)
    for upper in range(2):
        for middle in range(2):
            for inner in range(2):
                corner = 4 * upper + 2 * middle + inner
                row_index = (
                    brick_index[None, :] * (edge_cells * edge_cells * edge_cells)
                    + ((coord_x + upper) * edge_cells + (coord_y + middle)) * edge_cells
                    + (coord_z + inner)
                )
                gathered = jnp.take(flat_voxels, row_index, axis=0)
                total = (
                    total
                    + gathered.astype(jnp.float32) * weights[corner].astype(jnp.float32)[:, :, None]
                )
    return jnp.transpose(total, (2, 0, 1)).astype(jnp.bfloat16)


def shade(mixed_in, spacing_piece, w_in, w_mid, w_last, w_feat, w_density):
    channels, samples, extent = mixed_in.shape
    flat_in = mixed_in.reshape(channels, samples * extent)
    layer_one = jax.nn.relu(jnp.dot(w_in, flat_in, preferred_element_type=jnp.float32)).astype(
        jnp.bfloat16
    )
    layer_two = jax.nn.relu(jnp.dot(w_mid, layer_one, preferred_element_type=jnp.float32)).astype(
        jnp.bfloat16
    )
    layer_three = jax.nn.relu(
        jnp.dot(w_last, layer_two, preferred_element_type=jnp.float32)
    ).astype(jnp.bfloat16)
    colour = jnp.dot(w_feat, layer_three, preferred_element_type=jnp.float32).reshape(
        -1, samples, extent
    )
    density = jax.nn.softplus(
        jnp.dot(w_density, layer_three, preferred_element_type=jnp.float32)
    ).reshape(samples, extent)
    optical = density * spacing_piece.astype(jnp.float32)
    ahead_sum = jnp.cumsum(optical, axis=0) - optical
    weight = jnp.exp(-ahead_sum) * -jnp.expm1(-optical)
    return (jnp.sum(colour * weight[None], axis=1), jnp.sum(optical, axis=0))


def blocked(kernel, inputs, block_size):
    total_cols = inputs[0].shape[-1]
    steps_count = total_cols // block_size

    def one_block(block_index):
        block_start = block_index * block_size
        pieces = tuple(
            (
                lax.dynamic_slice_in_dim(member, block_start, block_size, member.ndim - 1)
                for member in inputs
            )
        )
        return kernel(*pieces)

    results = lax.map(one_block, jnp.arange(steps_count, dtype=jnp.int32))
    return tuple(
        (
            jnp.moveaxis(portion, 0, -2).reshape(portion.shape[1:-1] + (total_cols,))
            for portion in results
        )
    )


def spread_exact(values, placing):
    return jnp.dot(
        values, placing, preferred_element_type=jnp.float32, precision=lax.Precision.HIGHEST
    )


def collect_exact(values, placing):
    return lax.dot_general(
        values, placing, (((1,), (1,)), ((), ())), preferred_element_type=jnp.float32
    )


def on_device(
    bricks,
    brick_owner,
    brick_slot,
    sample_base,
    corner_weights,
    spacing,
    w_in,
    w_mid,
    w_last,
    w_feat,
    w_density,
):
    col_count = lax.axis_size("cols")
    ray_count = brick_slot.shape[1]
    samples = sample_base.shape[1]
    channels = bricks.shape[3] // EDGE
    capacity = max(2, 2 * ray_count // col_count)
    slot_count = col_count * capacity
    slot_block = min(slot_count, 256)
    ray_block = min(ray_count, 2048)
    flat_voxels = bricks[0].reshape(-1, channels)
    owners = brick_owner[0, :, 0]
    ray_iota = jnp.arange(ray_count, dtype=jnp.int32)
    same_owner = owners[:, None] == owners[None, :]
    earlier = ray_iota[None, :] < ray_iota[:, None]
    ranking = jnp.sum(jnp.logical_and(same_owner, earlier).astype(jnp.int32), axis=1)
    position = owners * capacity + ranking
    placing_mask = position[:, None] == jnp.arange(slot_count, dtype=jnp.int32)[None, :]
    placing_exact = placing_mask.astype(jnp.float32)
    placing_half = placing_mask.astype(jnp.bfloat16)
    requests = jnp.concatenate([brick_slot[0][None, :], sample_base[0]], axis=0).astype(jnp.float32)
    sent_ids = spread_exact(requests, placing_exact).astype(jnp.int32)
    sent_weights = jnp.dot(
        corner_weights[0].reshape(8 * samples, ray_count),
        placing_half,
        preferred_element_type=jnp.float32,
    ).astype(jnp.bfloat16)
    got_ids = lax.all_to_all(sent_ids, "cols", split_axis=1, concat_axis=1, tiled=True)

    def sampled(request_piece, weight_piece):
        return interpolate(
            flat_voxels,
            request_piece[0],
            request_piece[1:],
            weight_piece.reshape(8, samples, -1),
            EDGE,
        )

    def lit(mixed_in, spacing_piece):
        return shade(mixed_in, spacing_piece, w_in, w_mid, w_last, w_feat, w_density)

    got_weights = lax.all_to_all(sent_weights, "cols", split_axis=1, concat_axis=1, tiled=True)

    def sampled_tuple(request_piece, weight_piece):
        return (sampled(request_piece, weight_piece),)

    (mixed_slots,) = blocked(sampled_tuple, (got_ids, got_weights), slot_block)
    replied = lax.all_to_all(
        mixed_slots.reshape(channels * samples, slot_count),
        "cols",
        split_axis=1,
        concat_axis=1,
        tiled=True,
    )
    mixed_here = (
        collect_exact(replied, placing_half)
        .astype(jnp.bfloat16)
        .reshape(channels, samples, ray_count)
    )
    colour_here, depth_here = blocked(lit, (mixed_here, spacing[0]), ray_block)
    ahead_depth = jnp.zeros_like(depth_here)
    moving = depth_here
    for handoff_step in range(lax.axis_size("depth") - 1):
        moving = shifted(moving, "depth", 1)
        ahead_depth = ahead_depth + moving
    visible = jnp.exp(-ahead_depth)
    image_rows = lax.psum_scatter(
        visible[None, :] * colour_here, "depth", scatter_dimension=0, tiled=True
    )
    return (image_rows, visible[None, :])


def solution(mesh):
    in_specs = (
        P("depth", "cols", None, None),
        P("depth", "cols", None),
        P("depth", "cols"),
        P("depth", None, "cols"),
        P("depth", None, None, "cols"),
        P("depth", None, "cols"),
        P(),
        P(),
        P(),
        P(),
        P(),
    )
    out_specs = (P("depth", "cols"), P("depth", "cols"))
    return jax.shard_map(
        on_device, mesh=mesh, in_specs=in_specs, out_specs=out_specs, check_vma=False
    )
```

profile of v0, /device:TPU:1, one launch (start us, length us, event | category | flops | bytes accessed | tf_op | source)
XLA Modules:
  0.0 1545.1 jit_solution(12946136634902456078)
XLA Ops:
  62.5 1340.2 %while.18 = (s32[]{:T(128)}, bf16[8,32,16,256]{1,3,2,0:T(8,128)(2,1)}, s32[8]{0:T(128)}, s32[17,2048]{1,0:T(8,128)}, bf16[16384,32]{1,0:T(8,128)(2,1)}, /*index=...) while((s32[]{:T(128)}, ...), condition=%wide.region_2.4_spmd, body=%wide.region_1.3_spmd.sunk | while | flops 4940046 | bytes 12989315 | solution.py:78
  68.9 13.8 gather_fusion
  82.7 13.8 gather_fusion.1
  96.5 13.7 gather_fusion.2
  110.3 17.1 %gather_fusion.3 = bf16[4096,32]{1,0:T(8,128)(2,1)} fusion(bf16[16384,32]{1,0:T(8,128)(2,1)} %get-tuple-element.357, s32[4096]{0:T(1024)S(1)} %broadcast_clamp_fusion.19), kind=kCustom, calls=%fused_computation.4.clone.clone.1 | custom fusion | bytes 540672 | tf_op jit(solution)/shard_map/while/body/eval_jaxpr/jit(_take)/gather | solution.py:32
  127.4 17.1 %gather_fusion.4 = bf16[4096,32]{1,0:T(8,128)(2,1)} fusion(bf16[16384,32]{1,0:T(8,128)(2,1)} %get-tuple-element.357, s32[4096]{0:T(1024)S(1)} %broadcast_clamp_fusion.20), kind=kCustom, calls=%fused_computation.3.clone.clone.1 | custom fusion | bytes 540672 | tf_op jit(solution)/shard_map/while/body/eval_jaxpr/jit(_take)/gather | solution.py:32
  144.4 17.1 %gather_fusion.5 = bf16[4096,32]{1,0:T(8,128)(2,1)} fusion(bf16[16384,32]{1,0:T(8,128)(2,1)} %get-tuple-element.357, s32[4096]{0:T(1024)S(1)} %broadcast_clamp_fusion.21), kind=kCustom, calls=%fused_computation.2.clone.clone.1 | custom fusion | bytes 540672 | tf_op jit(solution)/shard_map/while/body/eval_jaxpr/jit(_take)/gather | solution.py:32
  161.5 17.1 %gather_fusion.6 = bf16[4096,32]{1,0:T(8,128)(2,1)} fusion(bf16[16384,32]{1,0:T(8,128)(2,1)} %get-tuple-element.357, s32[4096]{0:T(1024)S(1)} %broadcast_clamp_fusion.22), kind=kCustom, calls=%fused_computation.1.clone.clone.1 | custom fusion | bytes 540672 | tf_op jit(solution)/shard_map/while/body/eval_jaxpr/jit(_take)/gather | solution.py:32
  178.6 17.0 %gather_fusion.7 = bf16[4096,32]{1,0:T(8,128)(2,1)} fusion(bf16[16384,32]{1,0:T(8,128)(2,1)} %get-tuple-element.357, s32[4096]{0:T(1024)S(1)} %broadcast_clamp_fusion.23), kind=kCustom, calls=%fused_computation.clone.clone.1 | custom fusion | bytes 540672 | tf_op jit(solution)/shard_map/while/body/eval_jaxpr/jit(_take)/gather | solution.py:32
  236.5 13.8 gather_fusion
  250.4 13.8 gather_fusion.1
  264.2 13.7 gather_fusion.2
  278.0 17.1 %gather_fusion.3 = bf16[4096,32]{1,0:T(8,128)(2,1)} fusion(bf16[16384,32]{1,0:T(8,128)(2,1)} %get-tuple-element.357, s32[4096]{0:T(1024)S(1)} %broadcast_clamp_fusion.19), kind=kCustom, calls=%fused_computation.4.clone.clone.1 | custom fusion | bytes 540672 | tf_op jit(solution)/shard_map/while/body/eval_jaxpr/jit(_take)/gather | solution.py:32
  295.0 17.1 %gather_fusion.4 = bf16[4096,32]{1,0:T(8,128)(2,1)} fusion(bf16[16384,32]{1,0:T(8,128)(2,1)} %get-tuple-element.357, s32[4096]{0:T(1024)S(1)} %broadcast_clamp_fusion.20), kind=kCustom, calls=%fused_computation.3.clone.clone.1 | custom fusion | bytes 540672 | tf_op jit(solution)/shard_map/while/body/eval_jaxpr/jit(_take)/gather | solution.py:32
  312.1 17.1 %gather_fusion.5 = bf16[4096,32]{1,0:T(8,128)(2,1)} fusion(bf16[16384,32]{1,0:T(8,128)(2,1)} %get-tuple-element.357, s32[4096]{0:T(1024)S(1)} %broadcast_clamp_fusion.21), kind=kCustom, calls=%fused_computation.2.clone.clone.1 | custom fusion | bytes 540672 | tf_op jit(solution)/shard_map/while/body/eval_jaxpr/jit(_take)/gather | solution.py:32
  329.2 17.1 %gather_fusion.6 = bf16[4096,32]{1,0:T(8,128)(2,1)} fusion(bf16[16384,32]{1,0:T(8,128)(2,1)} %get-tuple-element.357, s32[4096]{0:T(1024)S(1)} %broadcast_clamp_fusion.22), kind=kCustom, calls=%fused_computation.1.clone.clone.1 | custom fusion | bytes 540672 | tf_op jit(solution)/shard_map/while/body/eval_jaxpr/jit(_take)/gather | solution.py:32
  346.3 17.0 %gather_fusion.7 = bf16[4096,32]{1,0:T(8,128)(2,1)} fusion(bf16[16384,32]{1,0:T(8,128)(2,1)} %get-tuple-element.357, s32[4096]{0:T(1024)S(1)} %broadcast_clamp_fusion.23), kind=kCustom, calls=%fused_computation.clone.clone.1 | custom fusion | bytes 540672 | tf_op jit(solution)/shard_map/while/body/eval_jaxpr/jit(_take)/gather | solution.py:32
  404.0 13.8 gather_fusion
  417.8 13.8 gather_fusion.1
  431.6 13.7 gather_fusion.2
  445.4 17.1 %gather_fusion.3 = bf16[4096,32]{1,0:T(8,128)(2,1)} fusion(bf16[16384,32]{1,0:T(8,128)(2,1)} %get-tuple-element.357, s32[4096]{0:T(1024)S(1)} %broadcast_clamp_fusion.19), kind=kCustom, calls=%fused_computation.4.clone.clone.1 | custom fusion | bytes 540672 | tf_op jit(solution)/shard_map/while/body/eval_jaxpr/jit(_take)/gather | solution.py:32
  462.5 17.1 %gather_fusion.4 = bf16[4096,32]{1,0:T(8,128)(2,1)} fusion(bf16[16384,32]{1,0:T(8,128)(2,1)} %get-tuple-element.357, s32[4096]{0:T(1024)S(1)} %broadcast_clamp_fusion.20), kind=kCustom, calls=%fused_computation.3.clone.clone.1 | custom fusion | bytes 540672 | tf_op jit(solution)/shard_map/while/body/eval_jaxpr/jit(_take)/gather | solution.py:32
  479.6 17.1 %gather_fusion.5 = bf16[4096,32]{1,0:T(8,128)(2,1)} fusion(bf16[16384,32]{1,0:T(8,128)(2,1)} %get-tuple-element.357, s32[4096]{0:T(1024)S(1)} %broadcast_clamp_fusion.21), kind=kCustom, calls=%fused_computation.2.clone.clone.1 | custom fusion | bytes 540672 | tf_op jit(solution)/shard_map/while/body/eval_jaxpr/jit(_take)/gather | solution.py:32
  496.7 17.1 %gather_fusion.6 = bf16[4096,32]{1,0:T(8,128)(2,1)} fusion(bf16[16384,32]{1,0:T(8,128)(2,1)} %get-tuple-element.357, s32[4096]{0:T(1024)S(1)} %broadcast_clamp_fusion.22), kind=kCustom, calls=%fused_computation.1.clone.clone.1 | custom fusion | bytes 540672 | tf_op jit(solution)/shard_map/while/body/eval_jaxpr/jit(_take)/gather | solution.py:32
  513.8 17.0 %gather_fusion.7 = bf16[4096,32]{1,0:T(8,128)(2,1)} fusion(bf16[16384,32]{1,0:T(8,128)(2,1)} %get-tuple-element.357, s32[4096]{0:T(1024)S(1)} %broadcast_clamp_fusion.23), kind=kCustom, calls=%fused_computation.clone.clone.1 | custom fusion | bytes 540672 | tf_op jit(solution)/shard_map/while/body/eval_jaxpr/jit(_take)/gather | solution.py:32
  571.6 13.8 gather_fusion
  585.4 13.8 gather_fusion.1
  599.2 13.7 gather_fusion.2
  613.0 17.1 %gather_fusion.3 = bf16[4096,32]{1,0:T(8,128)(2,1)} fusion(bf16[16384,32]{1,0:T(8,128)(2,1)} %get-tuple-element.357, s32[4096]{0:T(1024)S(1)} %broadcast_clamp_fusion.19), kind=kCustom, calls=%fused_computation.4.clone.clone.1 | custom fusion | bytes 540672 | tf_op jit(solution)/shard_map/while/body/eval_jaxpr/jit(_take)/gather | solution.py:32
  630.1 17.1 %gather_fusion.4 = bf16[4096,32]{1,0:T(8,128)(2,1)} fusion(bf16[16384,32]{1,0:T(8,128)(2,1)} %get-tuple-element.357, s32[4096]{0:T(1024)S(1)} %broadcast_clamp_fusion.20), kind=kCustom, calls=%fused_computation.3.clone.clone.1 | custom fusion | bytes 540672 | tf_op jit(solution)/shard_map/while/body/eval_jaxpr/jit(_take)/gather | solution.py:32
  647.2 17.1 %gather_fusion.5 = bf16[4096,32]{1,0:T(8,128)(2,1)} fusion(bf16[16384,32]{1,0:T(8,128)(2,1)} %get-tuple-element.357, s32[4096]{0:T(1024)S(1)} %broadcast_clamp_fusion.21), kind=kCustom, calls=%fused_computation.2.clone.clone.1 | custom fusion | bytes 540672 | tf_op jit(solution)/shard_map/while/body/eval_jaxpr/jit(_take)/gather | solution.py:32
  664.3 17.1 %gather_fusion.6 = bf16[4096,32]{1,0:T(8,128)(2,1)} fusion(bf16[16384,32]{1,0:T(8,128)(2,1)} %get-tuple-element.357, s32[4096]{0:T(1024)S(1)} %broadcast_clamp_fusion.22), kind=kCustom, calls=%fused_computation.1.clone.clone.1 | custom fusion | bytes 540672 | tf_op jit(solution)/shard_map/while/body/eval_jaxpr/jit(_take)/gather | solution.py:32
  681.4 17.0 %gather_fusion.7 = bf16[4096,32]{1,0:T(8,128)(2,1)} fusion(bf16[16384,32]{1,0:T(8,128)(2,1)} %get-tuple-element.357, s32[4096]{0:T(1024)S(1)} %broadcast_clamp_fusion.23), kind=kCustom, calls=%fused_computation.clone.clone.1 | custom fusion | bytes 540672 | tf_op jit(solution)/shard_map/while/body/eval_jaxpr/jit(_take)/gather | solution.py:32
  739.2 13.8 gather_fusion
  753.1 13.8 gather_fusion.1
  780.6 17.1 %gather_fusion.3 = bf16[4096,32]{1,0:T(8,128)(2,1)} fusion(bf16[16384,32]{1,0:T(8,128)(2,1)} %get-tuple-element.357, s32[4096]{0:T(1024)S(1)} %broadcast_clamp_fusion.19), kind=kCustom, calls=%fused_computation.4.clone.clone.1 | custom fusion | bytes 540672 | tf_op jit(solution)/shard_map/while/body/eval_jaxpr/jit(_take)/gather | solution.py:32
  797.7 17.1 %gather_fusion.4 = bf16[4096,32]{1,0:T(8,128)(2,1)} fusion(bf16[16384,32]{1,0:T(8,128)(2,1)} %get-tuple-element.357, s32[4096]{0:T(1024)S(1)} %broadcast_clamp_fusion.20), kind=kCustom, calls=%fused_computation.3.clone.clone.1 | custom fusion | bytes 540672 | tf_op jit(solution)/shard_map/while/body/eval_jaxpr/jit(_take)/gather | solution.py:32
  814.8 17.1 %gather_fusion.5 = bf16[4096,32]{1,0:T(8,128)(2,1)} fusion(bf16[16384,32]{1,0:T(8,128)(2,1)} %get-tuple-element.357, s32[4096]{0:T(1024)S(1)} %broadcast_clamp_fusion.21), kind=kCustom, calls=%fused_computation.2.clone.clone.1 | custom fusion | bytes 540672 | tf_op jit(solution)/shard_map/while/body/eval_jaxpr/jit(_take)/gather | solution.py:32
  831.9 17.1 %gather_fusion.6 = bf16[4096,32]{1,0:T(8,128)(2,1)} fusion(bf16[16384,32]{1,0:T(8,128)(2,1)} %get-tuple-element.357, s32[4096]{0:T(1024)S(1)} %broadcast_clamp_fusion.22), kind=kCustom, calls=%fused_computation.1.clone.clone.1 | custom fusion | bytes 540672 | tf_op jit(solution)/shard_map/while/body/eval_jaxpr/jit(_take)/gather | solution.py:32
  849.0 17.0 %gather_fusion.7 = bf16[4096,32]{1,0:T(8,128)(2,1)} fusion(bf16[16384,32]{1,0:T(8,128)(2,1)} %get-tuple-element.357, s32[4096]{0:T(1024)S(1)} %broadcast_clamp_fusion.23), kind=kCustom, calls=%fused_computation.clone.clone.1 | custom fusion | bytes 540672 | tf_op jit(solution)/shard_map/while/body/eval_jaxpr/jit(_take)/gather | solution.py:32
  906.6 13.8 gather_fusion
  920.5 13.8 gather_fusion.1
  934.3 13.7 gather_fusion.2
  948.1 17.1 %gather_fusion.3 = bf16[4096,32]{1,0:T(8,128)(2,1)} fusion(bf16[16384,32]{1,0:T(8,128)(2,1)} %get-tuple-element.357, s32[4096]{0:T(1024)S(1)} %broadcast_clamp_fusion.19), kind=kCustom, calls=%fused_computation.4.clone.clone.1 | custom fusion | bytes 540672 | tf_op jit(solution)/shard_map/while/body/eval_jaxpr/jit(_take)/gather | solution.py:32
  965.1 17.1 %gather_fusion.4 = bf16[4096,32]{1,0:T(8,128)(2,1)} fusion(bf16[16384,32]{1,0:T(8,128)(2,1)} %get-tuple-element.357, s32[4096]{0:T(1024)S(1)} %broadcast_clamp_fusion.20), kind=kCustom, calls=%fused_computation.3.clone.clone.1 | custom fusion | bytes 540672 | tf_op jit(solution)/shard_map/while/body/eval_jaxpr/jit(_take)/gather | solution.py:32
  982.2 17.1 %gather_fusion.5 = bf16[4096,32]{1,0:T(8,128)(2,1)} fusion(bf16[16384,32]{1,0:T(8,128)(2,1)} %get-tuple-element.357, s32[4096]{0:T(1024)S(1)} %broadcast_clamp_fusion.21), kind=kCustom, calls=%fused_computation.2.clone.clone.1 | custom fusion | bytes 540672 | tf_op jit(solution)/shard_map/while/body/eval_jaxpr/jit(_take)/gather | solution.py:32
  999.3 17.1 %gather_fusion.6 = bf16[4096,32]{1,0:T(8,128)(2,1)} fusion(bf16[16384,32]{1,0:T(8,128)(2,1)} %get-tuple-element.357, s32[4096]{0:T(1024)S(1)} %broadcast_clamp_fusion.22), kind=kCustom, calls=%fused_computation.1.clone.clone.1 | custom fusion | bytes 540672 | tf_op jit(solution)/shard_map/while/body/eval_jaxpr/jit(_take)/gather | solution.py:32
  1016.4 17.0 %gather_fusion.7 = bf16[4096,32]{1,0:T(8,128)(2,1)} fusion(bf16[16384,32]{1,0:T(8,128)(2,1)} %get-tuple-element.357, s32[4096]{0:T(1024)S(1)} %broadcast_clamp_fusion.23), kind=kCustom, calls=%fused_computation.clone.clone.1 | custom fusion | bytes 540672 | tf_op jit(solution)/shard_map/while/body/eval_jaxpr/jit(_take)/gather | solution.py:32
  1074.3 13.8 gather_fusion
  1088.1 13.8 gather_fusion.1
  1115.7 17.1 %gather_fusion.3 = bf16[4096,32]{1,0:T(8,128)(2,1)} fusion(bf16[16384,32]{1,0:T(8,128)(2,1)} %get-tuple-element.357, s32[4096]{0:T(1024)S(1)} %broadcast_clamp_fusion.19), kind=kCustom, calls=%fused_computation.4.clone.clone.1 | custom fusion | bytes 540672 | tf_op jit(solution)/shard_map/while/body/eval_jaxpr/jit(_take)/gather | solution.py:32
  1132.8 17.1 %gather_fusion.4 = bf16[4096,32]{1,0:T(8,128)(2,1)} fusion(bf16[16384,32]{1,0:T(8,128)(2,1)} %get-tuple-element.357, s32[4096]{0:T(1024)S(1)} %broadcast_clamp_fusion.20), kind=kCustom, calls=%fused_computation.3.clone.clone.1 | custom fusion | bytes 540672 | tf_op jit(solution)/shard_map/while/body/eval_jaxpr/jit(_take)/gather | solution.py:32
  1149.9 17.1 %gather_fusion.5 = bf16[4096,32]{1,0:T(8,128)(2,1)} fusion(bf16[16384,32]{1,0:T(8,128)(2,1)} %get-tuple-element.357, s32[4096]{0:T(1024)S(1)} %broadcast_clamp_fusion.21), kind=kCustom, calls=%fused_computation.2.clone.clone.1 | custom fusion | bytes 540672 | tf_op jit(solution)/shard_map/while/body/eval_jaxpr/jit(_take)/gather | solution.py:32
  1167.0 17.1 %gather_fusion.6 = bf16[4096,32]{1,0:T(8,128)(2,1)} fusion(bf16[16384,32]{1,0:T(8,128)(2,1)} %get-tuple-element.357, s32[4096]{0:T(1024)S(1)} %broadcast_clamp_fusion.22), kind=kCustom, calls=%fused_computation.1.clone.clone.1 | custom fusion | bytes 540672 | tf_op jit(solution)/shard_map/while/body/eval_jaxpr/jit(_take)/gather | solution.py:32
  1184.1 17.0 %gather_fusion.7 = bf16[4096,32]{1,0:T(8,128)(2,1)} fusion(bf16[16384,32]{1,0:T(8,128)(2,1)} %get-tuple-element.357, s32[4096]{0:T(1024)S(1)} %broadcast_clamp_fusion.23), kind=kCustom, calls=%fused_computation.clone.clone.1 | custom fusion | bytes 540672 | tf_op jit(solution)/shard_map/while/body/eval_jaxpr/jit(_take)/gather | solution.py:32
  1241.7 13.8 gather_fusion
  1255.5 13.8 gather_fusion.1
  1283.1 17.1 %gather_fusion.3 = bf16[4096,32]{1,0:T(8,128)(2,1)} fusion(bf16[16384,32]{1,0:T(8,128)(2,1)} %get-tuple-element.357, s32[4096]{0:T(1024)S(1)} %broadcast_clamp_fusion.19), kind=kCustom, calls=%fused_computation.4.clone.clone.1 | custom fusion | bytes 540672 | tf_op jit(solution)/shard_map/while/body/eval_jaxpr/jit(_take)/gather | solution.py:32
  1300.2 17.1 %gather_fusion.4 = bf16[4096,32]{1,0:T(8,128)(2,1)} fusion(bf16[16384,32]{1,0:T(8,128)(2,1)} %get-tuple-element.357, s32[4096]{0:T(1024)S(1)} %broadcast_clamp_fusion.20), kind=kCustom, calls=%fused_computation.3.clone.clone.1 | custom fusion | bytes 540672 | tf_op jit(solution)/shard_map/while/body/eval_jaxpr/jit(_take)/gather | solution.py:32
  1317.3 17.1 %gather_fusion.5 = bf16[4096,32]{1,0:T(8,128)(2,1)} fusion(bf16[16384,32]{1,0:T(8,128)(2,1)} %get-tuple-element.357, s32[4096]{0:T(1024)S(1)} %broadcast_clamp_fusion.21), kind=kCustom, calls=%fused_computation.2.clone.clone.1 | custom fusion | bytes 540672 | tf_op jit(solution)/shard_map/while/body/eval_jaxpr/jit(_take)/gather | solution.py:32
  1334.4 17.1 %gather_fusion.6 = bf16[4096,32]{1,0:T(8,128)(2,1)} fusion(bf16[16384,32]{1,0:T(8,128)(2,1)} %get-tuple-element.357, s32[4096]{0:T(1024)S(1)} %broadcast_clamp_fusion.22), kind=kCustom, calls=%fused_computation.1.clone.clone.1 | custom fusion | bytes 540672 | tf_op jit(solution)/shard_map/while/body/eval_jaxpr/jit(_take)/gather | solution.py:32
  1351.5 17.0 %gather_fusion.7 = bf16[4096,32]{1,0:T(8,128)(2,1)} fusion(bf16[16384,32]{1,0:T(8,128)(2,1)} %get-tuple-element.357, s32[4096]{0:T(1024)S(1)} %broadcast_clamp_fusion.23), kind=kCustom, calls=%fused_computation.clone.clone.1 | custom fusion | bytes 540672 | tf_op jit(solution)/shard_map/while/body/eval_jaxpr/jit(_take)/gather | solution.py:32
  1424.8 55.2 %all_to_all.36 = bf16[512,64,32]{0,2,1:T(8,128)(2,1)S(1)} all-to-all(bf16[512,64,32]{0,2,1:T(8,128)(2,1)S(1)} %copy.33), channel_id=1, replica_groups=mesh['depth'=4,'cols'=64] {'cols'}, dimensions={1} | all-to-all | bytes 4194304 | tf_op jit(solution)/shard_map/all_to_all | solution.py:157
  1518.1 20.2 %reduce-scatter.4.cloned.1.call-done = f32[32,1024]{1,0:T(8,128)} async-done(((f32[128,1024]{1,0:T(8,128)}), f32[32,1024]{1,0:T(8,128)}) %reduce-scatter.4.cloned.1.call-update) | async-done | bytes 131088
  (394 shorter events, 477.3 us)
Async XLA Ops:
  7.2 20.2 %copy-start = (bf16[1,8,16,1024]{3,2,1,0:T(8,128)(2,1)S(1)}, bf16[1,8,16,1024]{3,2,1,0:T(8,128)(2,1)}, u32[]{:S(2)}) copy-start(bf16[1,8,16,1024]{3,2,1,0:T(8,128)(2,1)} %param.19) | copy-start | bytes 786436
  9.2 20.5 %copy-start.7 = (s32[1024]{0:T(1024)}, s32[1024]{0:T(1024)S(1)}, u32[]{:S(2)}) copy-start(s32[1024]{0:T(1024)S(1)} %multiply_add_fusion.4) | copy-start | bytes 12292
  13.3 31.2 %copy-start.2 = (bf16[1,4,256,512]{3,2,1,0:T(8,128)(2,1)S(1)}, bf16[1,4,256,512]{3,2,1,0:T(8,128)(2,1)}, u32[]{:S(2)}) copy-start(bf16[1,4,256,512]{3,2,1,0:T(8,128)(2,1)} %param.15) | copy-start | bytes 3145732
  14.3 24.7 %all-to-all-start = ((s32[64,1,544]{2,1,0:T(1,128)}), s32[64,1,544]{2,1,0:T(1,128)S(1)}, u32[]{:S(2)}, u32[]{:S(2)}) async-start(s32[64,1,544]{2,1,0:T(1,128)} %reshape.240), calls=%async_computation | async-start | bytes 327680 | tf_op jit(solution)/shard_map/all_to_all | solution.py:137
  39.0 23.0 %all-to-all-start.1 = ((bf16[128,64,32]{0,2,1:T(8,128)(2,1)}), bf16[128,64,32]{0,2,1:T(8,128)(2,1)}, u32[]{:S(2)}, u32[]{:S(2)}) async-start(bf16[128,64,32]{0,2,1:T(8,128)(2,1)} %bitcast.16), calls=%async_computation.1 | async-start | bytes 1048576 | tf_op jit(solution)/shard_map/all_to_all | solution.py:151
  44.3 1494.0 %reduce-scatter.4.cloned.1.call-start = ((), (), s32[]{:S(2)}) async-start(), calls=%async_computation.4 | async-start | bytes 655360
  1424.7 55.2 %copy-start.8 = (s32[1024]{0:T(1024)S(1)}, s32[1024]{0:T(1024)}, u32[]{:S(2)}) copy-start(s32[1024]{0:T(1024)} %copy-done.7) | copy-start | bytes 12292
  1479.9 3.2 copy-start.10
  1479.9 3.2 copy-start.11
  1482.6 4.7 copy-start.4
  1487.3 5.4 copy-start.9
  1490.8 2.0 copy-start.1
  1492.7 1.3 copy-start.3
  1492.7 4.6 copy-start.5
  1494.1 10.0 collective-permute-start
  1504.1 3.9 collective-permute-start.1
  1508.0 8.9 collective-permute-start.2
  1516.9 21.4 %copy-start.6 = (f32[1024]{0:T(1024)}, f32[1024]{0:T(1024)S(1)}, u32[]{:S(2)}) copy-start(f32[1024]{0:T(1024)S(1)} %negate_exponential_fusion) | copy-start | bytes 12292
Sparse Core Ops, SparseCore 0:
  1518.3 19.9 reduce-scatter.3
where the time goes:
time: 1560 us; the launch traced here: 1550 us
  local copies, waits for them, and re-layouts  1150 us (74%)
  other arithmetic  223 us (14%)
  blocking collectives  55.2 us (4%)
  waiting for transfers between devices  41 us (3%)
  starting transfers between devices  28.5 us (2%)
  matrix products  24.1 us (2%)
    gather x64, local copies, waits for them, and re-layouts, interpolate(): gathered = jnp.take(flat_voxels, row_index, axis=0)  1010 us
    dynamic_update_slice x8, other arithmetic, blocked(): results = lax.map(one_block, jnp.arange(steps_count, dtype=jnp.int32))  103 us
    while x128, local copies, waits for them, and re-layouts  78.9 us
    convert_element_type x64, other arithmetic, interpolate(): weights[corner].astype(jnp.float32)[:, :, None]  63.2 us
    all_to_all x1, blocking collectives, on_device(): lax.all_to_all(mixed_slots.reshape(channels * samples, slot_count), 'cols...  55.2 us
    and x24, other arithmetic, interpolate(): gathered = jnp.take(flat_voxels, row_index, axis=0)  35 us
  transfers between devices with their start and end apart: 6, of which 4 were waited for; matrix products, arithmetic and copies ran while one was open for 1% of the time, Pallas kernels for 0%

commit v1 on v0

v1 whole, which is shorter than its diff:
```python
import functools

import jax
import jax.numpy as jnp
from jax import lax
from jax.experimental import pallas as pl
from jax.experimental.pallas import tpu as pltpu
from jax.sharding import PartitionSpec as P

EDGE = 16
LINES = EDGE * EDGE
CH = 32
S = 16
HID = 128
COLS = 64
CAP = 32
HALF = CAP // 2
ROWS = 48
RAYS = 1024
SLOTS = COLS * CAP
TILE = 128
MAX_TILES = SLOTS // TILE + 3
POS = EDGE - 1
WIDE = 256
F32 = jnp.float32
BF16 = jnp.bfloat16


def iota(shape, dim, dtype=jnp.int32):
    return lax.broadcasted_iota(jnp.int32, shape, dim).astype(dtype)


def one_hot(mask):
    return jnp.where(mask, 1.0, 0.0).astype(BF16)


def dot(a, b):
    return jnp.dot(a, b, preferred_element_type=F32)


def dot_rows(a, b):
    return lax.dot_general(a, b, (((1,), (1,)), ((), ())), preferred_element_type=F32)


def ask_kernel(owner_ref, slot_ref, base_ref, weight_ref, spacing_ref, sent_ref, place_ref):
    owner = owner_ref[...]
    mine = iota((COLS, RAYS), 0) == owner
    earlier = one_hot(iota((RAYS, RAYS), 0) < iota((RAYS, RAYS), 1))
    count = dot(one_hot(mine), earlier)
    rank = jnp.sum(jnp.where(mine, count, 0.0), axis=0, keepdims=True).astype(jnp.int32)
    place = owner * CAP + rank
    place_ref[...] = place
    sent = dot_rows(one_hot(iota((SLOTS, RAYS), 0) == place), weight_ref[...])
    sent_ref[:, :CAP, :] = sent.astype(BF16).reshape(COLS, CAP, HID)
    base = base_ref[...].astype(F32) + 0.5
    side = EDGE - 1
    coord_x = jnp.floor(base * (1.0 / (side * side)))
    rest = base - coord_x * (side * side)
    coord_y = jnp.floor(rest * (1.0 / side))
    coord_z = rest - coord_y * side - 0.5
    line = coord_x * EDGE + coord_y
    slot = slot_ref[...].astype(F32) + 1.0
    slot_rows = jnp.where(iota((S, RAYS), 0) == 0, slot, 0.0)
    features = jnp.concatenate([line, coord_z, spacing_ref[...].astype(F32), slot_rows], axis=0)
    second = rank >= HALF
    both = jnp.concatenate(
        [jnp.where(second, 0.0, features), jnp.where(second, features, 0.0)], axis=0
    ).astype(BF16)
    row = owner * HALF + jnp.where(second, rank - HALF, rank)
    sent = dot_rows(one_hot(iota((COLS * HALF, RAYS), 0) == row), both)
    sent_ref[:, CAP:, :] = sent.astype(BF16).reshape(COLS, HALF, HID)


def field_kernel(
    got_ref,
    brick_ref,
    w_in_ref,
    w_mid_ref,
    w_last_ref,
    w_feat_ref,
    w_density_ref,
    colour_ref,
    depth_ref,
    table_ref,
    pos_ref,
    weight_ref,
    feature_ref,
    mix_ref,
    mixed_ref,
    hidden_ref,
    density_ref,
    reply_ref,
):
    half = COLS * HALF
    second = got_ref[:, CAP:, :].reshape(half, HID)
    lane = iota((half, HID), 1)
    table_ref[:half, :HID] = got_ref[:, :HALF, :].reshape(half, HID)
    table_ref[half:, :HID] = got_ref[:, HALF:CAP, :].reshape(half, HID)
    zero = jnp.zeros((half, HID), BF16)
    table_ref[:half, HID:] = jnp.where(lane < HID // 2, second, zero)
    table_ref[half:, HID:] = jnp.where(lane < HID // 2, zero, second)

    pick_row = iota((16, HID), 0)
    pick_lane = iota((16, HID), 1)
    picks = one_hot(pick_lane == jnp.where(pick_row < 2, 3 * S + pick_row * (HID // 2), -1))
    keys = dot_rows(picks, second)
    key = jnp.concatenate([keys[0:1], keys[1:2]], axis=1) - 1.0
    member = jnp.where(iota((8, SLOTS), 0, F32) == key, 1.0, 0.0)
    chunks = SLOTS // 128
    stacked = jnp.concatenate([member[:, c * 128 : (c + 1) * 128] for c in range(chunks)], axis=0)
    before = one_hot(iota((128, 128), 0) < iota((128, 128), 1))
    inner = dot(stacked.astype(BF16), before)
    totals = jnp.sum(stacked, axis=1, keepdims=True)
    carry = jnp.zeros((8, 1), F32)
    pieces = []
    for c in range(chunks):
        pieces.append(inner[c * 8 : (c + 1) * 8] + carry)
        carry = carry + totals[c * 8 : (c + 1) * 8]
    counted = jnp.concatenate(pieces, axis=1)
    tiles = jnp.floor((carry + (TILE - 1.0)) * (1.0 / TILE))
    row = iota((8, 1), 0)
    starts = [jnp.sum(jnp.where(row < q, tiles, 0.0)) for q in range(1, 5)]
    first = jnp.where(row == 1, starts[0], jnp.where(row == 2, starts[1], starts[2]))
    first = jnp.where(row == 0, 0.0, first)
    pos = jnp.sum(member * (counted + first * TILE), axis=0, keepdims=True)
    pos = jnp.where(jnp.sum(member, axis=0, keepdims=True) > 0.0, pos, -1.0)
    pos_ref[...] = jnp.broadcast_to(pos, (8, SLOTS))
    limit1, limit2, limit3, tile_count = [start.astype(jnp.int32) for start in starts]
    reply_ref[...] = jnp.zeros_like(reply_ref)

    def one_tile(tile, carried):
        brick = (
            (tile >= limit1).astype(jnp.int32)
            + (tile >= limit2).astype(jnp.int32)
            + (tile >= limit3).astype(jnp.int32)
        )
        local = pos_ref[0:1, :] - (tile * TILE).astype(F32)
        chosen = one_hot(iota((TILE, SLOTS), 0, F32) == local)
        rays = dot(chosen, table_ref[...]).T
        weight_ref[...] = rays[:HID]
        feature_ref[...] = rays[HID : HID + HID // 2] + rays[HID + HID // 2 :]

        for s in range(S):
            lanes = slice(s * TILE, (s + 1) * TILE)
            line = feature_ref[s : s + 1, :]
            coord_x = jnp.floor(line * (1.0 / EDGE))
            coord_y = line - coord_x * EDGE
            rows = iota((EDGE, TILE), 0, F32)
            near = rows == coord_y
            far = rows == coord_y + 1.0
            x_full = jnp.broadcast_to(coord_x, (EDGE, TILE)).astype(BF16)
            none = jnp.zeros((EDGE, TILE), BF16)
            for e in range(2):
                parts = []
                for a in range(2):
                    low = weight_ref[(4 * a + e) * S + s : (4 * a + e) * S + s + 1, :]
                    high = weight_ref[(4 * a + 2 + e) * S + s : (4 * a + 2 + e) * S + s + 1, :]
                    parts.append(jnp.where(near, low, jnp.where(far, high, 0.0)).astype(BF16))
                for x in range(EDGE):
                    value = jnp.where(x_full == x, parts[0], none)
                    if x > 0:
                        value = jnp.where(x_full == x - 1, parts[1], value)
                    mix_ref[e * LINES + x * EDGE : e * LINES + (x + 1) * EDGE, lanes] = value
        for group in range(S * TILE // WIDE):
            lanes = slice(group * WIDE, (group + 1) * WIDE)
            spread = dot(brick_ref[brick], mix_ref[:, lanes])
            each = WIDE // TILE
            coord_z = jnp.concatenate(
                [feature_ref[S + each * group + i : S + each * group + i + 1, :] for i in range(each)],
                axis=1,
            )
            mixed = jnp.zeros((CH, WIDE), F32)
            for p in range(POS):
                mixed = jnp.where(coord_z == float(p), spread[p * CH : (p + 1) * CH], mixed)
            mixed_ref[:, lanes] = mixed.astype(BF16)
        layer = mixed_ref[...]
        for w_ref in (w_in_ref, w_mid_ref, w_last_ref):
            layer = jnp.maximum(dot(w_ref[...], layer), 0.0).astype(BF16)
        hidden_ref[...] = layer
        thin = dot(w_density_ref[...], layer)
        for s in range(S):
            density_ref[s : s + 1, :] = thin[0:1, s * TILE : (s + 1) * TILE]

        density = density_ref[...]
        density = jnp.maximum(density, 0.0) + jnp.log1p(jnp.exp(-jnp.abs(density)))
        optical = density * feature_ref[2 * S : 3 * S, :]
        ahead = [jnp.zeros((1, TILE), F32)]
        for s in range(S):
            ahead.append(ahead[s] + optical[s : s + 1])
        clear = jnp.exp(-jnp.concatenate(ahead[:S], axis=0))
        share = clear * (1.0 - jnp.exp(-optical))
        total = jnp.zeros((HID, TILE), F32)
        for s in range(S):
            hidden = hidden_ref[:, s * TILE : (s + 1) * TILE].astype(F32)
            total = total + hidden * share[s : s + 1]
        high = total.astype(BF16)
        low = (total - high.astype(F32)).astype(BF16)
        colour = dot(w_feat_ref[...], high) + dot(w_feat_ref[...], low)
        thick = ahead[S]
        thick_high = thick.astype(BF16).astype(F32)
        thick_mid = (thick - thick_high).astype(BF16).astype(F32)
        thick_low = thick - thick_high - thick_mid
        extra = jnp.concatenate(
            [thick_high, thick_mid, thick_low, jnp.zeros((13, TILE), F32)], axis=0
        )
        result = jnp.concatenate([colour, extra], axis=0).astype(BF16)
        reply_ref[...] += dot(result, chosen)
        return carried

    lax.fori_loop(0, tile_count, one_tile, 0)
    for part in range(2):
        block = reply_ref[:HID, part * half : (part + 1) * half].T
        colour_ref[:, part * HALF : (part + 1) * HALF, :] = block.astype(BF16).reshape(
            COLS, HALF, HID
        )
    depth_ref[...] = reply_ref[HID : HID + 16, :].astype(BF16)


def collect_kernel(colour_ref, depth_ref, place_ref, out_ref):
    table = colour_ref[...].reshape(SLOTS, HID).astype(F32).T.astype(BF16)
    found = one_hot(iota((SLOTS, RAYS), 0) == place_ref[...])
    out_ref[:HID, :] = dot(table, found).astype(BF16)
    out_ref[HID:, :] = dot(depth_ref[...], found).astype(BF16)


def vmem(count):
    return [pl.BlockSpec(memory_space=pltpu.VMEM)] * count


def make_table(bricks):
    turned = jnp.transpose(bricks, (0, 2, 1))
    return jnp.concatenate([turned[:, : POS * CH], turned[:, CH:]], axis=2)


def run_field(got, table, w_in, w_mid, w_last, w_feat, w_density):
    return pl.pallas_call(
        field_kernel,
        out_shape=(
            jax.ShapeDtypeStruct((COLS, CAP, HID), BF16),
            jax.ShapeDtypeStruct((16, SLOTS), BF16),
        ),
        in_specs=vmem(7),
        out_specs=tuple(vmem(2)),
        scratch_shapes=[
            pltpu.VMEM((SLOTS, 2 * HID), BF16),
            pltpu.VMEM((8, SLOTS), F32),
            pltpu.VMEM((HID, TILE), F32),
            pltpu.VMEM((HID // 2, TILE), F32),
            pltpu.VMEM((2 * LINES, S * TILE), BF16),
            pltpu.VMEM((CH, S * TILE), BF16),
            pltpu.VMEM((HID, S * TILE), BF16),
            pltpu.VMEM((S, TILE), F32),
            pltpu.VMEM((HID + 16, SLOTS), F32),
        ],
        compiler_params=pltpu.CompilerParams(vmem_limit_bytes=48 << 20),
        name="field",
    )(got, table, w_in, w_mid, w_last, w_feat, jnp.pad(w_density, ((0, 15), (0, 0))))


def on_device(
    bricks,
    brick_owner,
    brick_slot,
    sample_base,
    corner_weights,
    spacing,
    w_in,
    w_mid,
    w_last,
    w_feat,
    w_density,
):
    params = pltpu.CompilerParams(vmem_limit_bytes=48 << 20)
    sent, place = pl.pallas_call(
        ask_kernel,
        out_shape=(
            jax.ShapeDtypeStruct((COLS, ROWS, HID), BF16),
            jax.ShapeDtypeStruct((1, RAYS), jnp.int32),
        ),
        in_specs=vmem(5),
        out_specs=tuple(vmem(2)),
        compiler_params=params,
        name="ask",
    )(
        brick_owner.reshape(1, RAYS),
        brick_slot,
        sample_base[0],
        corner_weights[0].reshape(HID, RAYS),
        spacing[0],
    )
    got = lax.all_to_all(sent, "cols", split_axis=0, concat_axis=0, tiled=True)
    table = make_table(bricks[0])
    colour, depth = run_field(got, table, w_in, w_mid, w_last, w_feat, w_density)
    return colour, depth, place


def finish(colour, depth, place):
    params = pltpu.CompilerParams(vmem_limit_bytes=48 << 20)
    depth = depth[:3].reshape(3, 2, COLS, HALF).transpose(2, 0, 1, 3).reshape(COLS, 3 * CAP)
    colour = lax.all_to_all(colour, "cols", split_axis=0, concat_axis=0, tiled=True)
    depth = lax.all_to_all(depth, "cols", split_axis=0, concat_axis=0, tiled=True)
    depth = depth.reshape(COLS, 3, CAP).transpose(1, 0, 2).reshape(3, SLOTS)
    depth = jnp.pad(depth, ((0, 13), (0, 0)))
    here = pl.pallas_call(
        collect_kernel,
        out_shape=jax.ShapeDtypeStruct((HID + 16, RAYS), BF16),
        in_specs=vmem(3),
        out_specs=vmem(1)[0],
        compiler_params=params,
        name="collect",
    )(colour, depth, place)
    regions = lax.axis_size("depth")
    rows = HID // regions
    out = jnp.concatenate(
        [
            here[:HID].reshape(regions, rows, RAYS),
            jnp.broadcast_to(here[HID:][None], (regions, 16, RAYS)),
        ],
        axis=1,
    )
    out = lax.all_to_all(out, "depth", split_axis=0, concat_axis=0, tiled=True)
    thick = jnp.sum(out[:, rows : rows + 3].astype(F32), axis=1)
    ahead = jnp.cumsum(thick, axis=0) - thick
    visible = jnp.exp(-ahead)
    image = jnp.sum(visible[:, None, :] * out[:, :rows].astype(F32), axis=0)
    me = lax.axis_index("depth")
    mine = jnp.sum(jnp.where(jnp.arange(regions)[:, None] == me, visible, 0.0), axis=0)
    return image, mine[None, :]


def whole(*args):
    return finish(*on_device(*args))


def solution(mesh):
    in_specs = (
        P("depth", "cols", None, None),
        P("depth", "cols", None),
        P("depth", "cols"),
        P("depth", None, "cols"),
        P("depth", None, None, "cols"),
        P("depth", None, "cols"),
        P(),
        P(),
        P(),
        P(),
        P(),
    )
    out_specs = (P("depth", "cols"), P("depth", "cols"))
    return jax.shard_map(
        whole, mesh=mesh, in_specs=in_specs, out_specs=out_specs, check_vma=False
    )
```

time: 1560 us -> 159 us (0.10)
  local copies, waits for them, and re-layouts: 1150 us -> 5.43 us
  other arithmetic: 223 us -> 2.4 us
  Pallas kernels: 0 us -> 58.8 us
  blocking collectives: 55.2 us -> 21.1 us
  matrix products: 24.1 us -> 0 us
    gather x64 -> x0, local copies, waits for them, and re-layouts: 1010 us -> none  [interpolate(): gathered = jnp.take(flat_voxels, row_index, axis=0)]
    dynamic_update_slice x8 -> x0, other arithmetic: 103 us -> none  [blocked(): results = lax.map(one_block, jnp.arange(steps_count, dtype=jnp.int32))]
    while x128 -> x0, local copies, waits for them, and re-layouts: 78.9 us -> none
    convert_element_type x64 -> x0, other arithmetic: 63.2 us -> none  [interpolate(): weights[corner].astype(jnp.float32)[:, :, None]]
    pallas_call x0 -> x3, Pallas kernels: none -> 58.8 us  [the longest x1 53.7 us: run_field(): pl.pallas_call(field_kernel, out_shape=(jax.ShapeDtypeStruct((COLS, CAP,...]
    and x24 -> x0, other arithmetic: 35 us -> none  [interpolate(): gathered = jnp.take(flat_voxels, row_index, axis=0)]
    all_to_all x1, blocking collectives: 55.2 us -> 21.1 us  [finish(): lax.all_to_all(depth, 'cols', split_axis=0, concat_axis=0, tiled=True)]
    all_to_all x2 -> x3, waiting for transfers between devices: 20.2 us -> 46.4 us  [the longest x1 21.7 us: on_device(): got = lax.all_to_all(sent, 'cols', split_axis=0, concat_axis=0, tiled=True)]
  transfers between devices with their start and end apart: 6 -> 3, of which waited for: 4 -> 3; matrix products, arithmetic and copies ran while one was open for 1% -> 1% of each run, Pallas kernels for 0% -> 0%
where the time goes in v1:
time: 159 us; the launch traced here: 158 us
  Pallas kernels  58.8 us (37%)
  waiting for transfers between devices  46.4 us (29%)
  starting transfers between devices  23.5 us (15%)
  blocking collectives  21.1 us (13%)
  local copies, waits for them, and re-layouts  5.43 us (3%)
  other arithmetic  2.4 us (2%)
    pallas_call x1, Pallas kernels, run_field(): pl.pallas_call(field_kernel, out_shape=(jax.ShapeDtypeStruct((COLS, CAP,...  53.7 us
    all_to_all x1, waiting for transfers between devices, on_device(): got = lax.all_to_all(sent, 'cols', split_axis=0, concat_axis=0, tiled=True)  21.7 us
    all_to_all x1, blocking collectives, finish(): lax.all_to_all(depth, 'cols', split_axis=0, concat_axis=0, tiled=True)  21.1 us
    all_to_all x1, waiting for transfers between devices, finish(): lax.all_to_all(colour, 'cols', split_axis=0, concat_axis=0, tiled=True)  17.5 us
    all_to_all x1, starting transfers between devices, on_device(): got = lax.all_to_all(sent, 'cols', split_axis=0, concat_axis=0, tiled=True)  13 us
    all_to_all x1, waiting for transfers between devices, finish(): out = lax.all_to_all(out, 'depth', split_axis=0, concat_axis=0, tiled=True)  7.17 us
    all_to_all x1, starting transfers between devices, finish(): out = lax.all_to_all(out, 'depth', split_axis=0, concat_axis=0, tiled=True)  5.82 us
    all_to_all x1, starting transfers between devices, finish(): lax.all_to_all(colour, 'cols', split_axis=0, concat_axis=0, tiled=True)  4.74 us
  transfers between devices with their start and end apart: 3, of which 3 were waited for; matrix products, arithmetic and copies ran while one was open for 1% of the time, Pallas kernels for 0%

profile of v1, /device:TPU:1, one launch (start us, length us, event | category | flops | bytes accessed | tf_op | source)
XLA Modules:
  0.0 158.5 jit_solution(17052097898163497784)
XLA Ops:
  0.6 0.0 copy-start
  0.6 0.9 copy-done
  1.6 0.0 copy-start.1
  1.6 0.8 copy-done.1
  2.4 0.0 copy-start.5
  2.4 0.8 copy-done.5
  3.2 0.0 copy-start.6
  3.2 0.7 copy-done.6
  3.9 0.0 copy-start.7
  3.9 0.7 copy-done.7
  4.6 0.0 copy-start.8
  4.6 0.0 copy-start.9
  4.6 0.0 copy-start.10
  4.6 3.1 %ask.1 = (bf16[64,48,128]{2,1,0:T(8,128)(2,1)}, s32[1,1024]{1,0:T(1,128)S(1)}) custom-call(s32[1,1024]{1,0:T(1,128)S(1)} %bitcast.17, s32[1,1024]{1,0:T(1,128)S(1)} %copy-done.7, s32[16,1024]{1,0:T(8,128)S(1)} %bitcast.15, bf16[128,1024]{1,0:T(8,128)(2,1)S(1)} %bitcast.14, bf16[16,1024]{1,0:T(8,128)(2,1)S(1)} %bitcast.16), custom_call_target="tpu_custom_call" | custom-call | tf_op jit(solution)/shard_map/ask/pallas_call | solution.py:274
  7.6 13.0 %all-to-all-start = ((bf16[64,48,128]{2,1,0:T(8,128)(2,1)}), bf16[64,48,128]{2,1,0:T(8,128)(2,1)S(1)}, u32[]{:S(2)}, u32[]{:S(2)}) async-start(bf16[64,48,128]{2,1,0:T(8,128)(2,1)} %get-tuple-element.6), calls=%async_computation | async-start | bytes 1572864 | tf_op jit(solution)/shard_map/all_to_all | solution.py:291
  20.6 0.0 copy-done.8
  20.6 0.5 copy.19
  21.2 0.0 copy-done.9
  21.2 0.1 copy.20.w_in_ref
  21.3 0.0 copy-done.10
  21.3 0.1 fusion
  21.5 0.0 copy-start.2
  21.5 0.0 copy-start.3
  21.5 0.0 copy-start.4
  21.5 0.2 pad_maximum_fusion.brick_ref
  21.7 21.7 %all-to-all-done.got_ref = bf16[64,48,128]{2,1,0:T(8,128)(2,1)S(1)} async-done(((bf16[64,48,128]{2,1,0:T(8,128)(2,1)}), bf16[64,48,128]{2,1,0:T(8,128)(2,1)S(1)}, u32[]{:S(2)}, u32[]{:S(2)}) %all-to-all-start) | async-done | bytes 786464 | tf_op jit(solution)/shard_map/all_to_all | solution.py:291
  43.4 0.0 copy-done.2
  43.4 0.0 copy-done.3
  43.4 0.0 copy-done.4
  43.4 53.7 %field.1 = (bf16[64,32,128]{2,1,0:T(8,128)(2,1)}, bf16[16,2048]{1,0:T(8,128)(2,1)S(1)}) custom-call(bf16[64,48,128]{2,1,0:T(8,128)(2,1)S(1)} %all-to-all-done.got_ref, bf16[4,480,512]{2,1,0:T(8,128)(2,1)S(1)} %pad_maximum_fusion.brick_ref, bf16[128,32]{1,0:T(8,128)(2,1)S(1)} %copy.20.w_in_ref, bf16[128,128]{1,0:T(8,128)(2,1)S(1)} %copy-done.2, ...), custom_call_target="tpu_custom_call" | custom-call | tf_op jit(solution)/shard_map/field/pallas_call | solution.py:236
  97.1 0.1 reshape.38
  97.2 0.1 copy.21
  97.3 0.1 copy.22
  97.4 21.1 %all_to_all.24 = bf16[64,1,96]{2,1,0:T(2,128)(2,1)S(1)} all-to-all(bf16[64,1,96]{2,1,0:T(2,128)(2,1)S(1)} %copy.22), channel_id=1, replica_groups=mesh['depth'=4,'cols'=64] {'cols'}, dimensions={0} | all-to-all | bytes 24576 | tf_op jit(solution)/shard_map/all_to_all | solution.py:301
  118.5 4.7 %all-to-all-start.1 = ((bf16[64,32,128]{2,1,0:T(8,128)(2,1)}), bf16[64,32,128]{2,1,0:T(8,128)(2,1)S(1)}, u32[]{:S(2)}, u32[]{:S(2)}) async-start(bf16[64,32,128]{2,1,0:T(8,128)(2,1)} %get-tuple-element.7), calls=%async_computation.1 | async-start | bytes 1048576 | tf_op jit(solution)/shard_map/all_to_all | solution.py:300
  123.3 0.1 copy.23
  123.4 0.1 copy.24
  123.5 0.1 reshape.40
  123.6 17.5 %all-to-all-done.1.colour_ref = bf16[64,32,128]{2,1,0:T(8,128)(2,1)S(1)} async-done(((bf16[64,32,128]{2,1,0:T(8,128)(2,1)}), bf16[64,32,128]{2,1,0:T(8,128)(2,1)S(1)}, u32[]{:S(2)}, u32[]{:S(2)}) %all-to-all-start.1) | async-done | bytes 524320 | tf_op jit(solution)/shard_map/all_to_all | solution.py:300
  141.1 2.1 %collect.1 = bf16[144,1024]{1,0:T(8,128)(2,1)S(1)} custom-call(bf16[64,32,128]{2,1,0:T(8,128)(2,1)S(1)} %all-to-all-done.1.colour_ref, bf16[16,2048]{1,0:T(8,128)(2,1)S(1)} %pad.9.depth_ref, s32[1,1024]{1,0:T(1,128)S(1)} %get-tuple-element.9.place_ref), custom_call_target="tpu_custom_call" | custom-call | tf_op jit(solution)/shard_map/collect/pallas_call | solution.py:304
  143.2 0.8 pad_maximum_fusion.1
  144.0 5.8 %all-to-all-start.3 = ((bf16[4,48,1024]{2,1,0:T(8,128)(2,1)}), bf16[4,48,1024]{2,1,0:T(8,128)(2,1)S(1)}, u32[]{:S(2)}, u32[]{:S(2)}) async-start(bf16[4,48,1024]{2,1,0:T(8,128)(2,1)} %pad_maximum_fusion.1), calls=%async_computation.3 | async-start | bytes 786432 | tf_op jit(solution)/shard_map/all_to_all | solution.py:321
  149.8 7.2 %all-to-all-done.3 = bf16[4,48,1024]{2,1,0:T(8,128)(2,1)S(1)} async-done(((bf16[4,48,1024]{2,1,0:T(8,128)(2,1)}), bf16[4,48,1024]{2,1,0:T(8,128)(2,1)S(1)}, u32[]{:S(2)}, u32[]{:S(2)}) %all-to-all-start.3) | async-done | bytes 393248 | tf_op jit(solution)/shard_map/all_to_all | solution.py:321
  157.1 0.7 select_reduce_fusion
  157.8 0.7 multiply_reduce_fusion
  (9 shorter events, 0.2 us)
Async XLA Ops:
  0.6 1.0 copy-start
  1.6 0.8 copy-start.1
  2.4 0.8 copy-start.5
  3.2 0.7 copy-start.6
  3.9 0.7 copy-start.7
  4.6 16.1 %copy-start.8 = (bf16[1,4,256,512]{3,2,1,0:T(8,128)(2,1)S(1)}, bf16[1,4,256,512]{3,2,1,0:T(8,128)(2,1)}, u32[]{:S(2)}) copy-start(bf16[1,4,256,512]{3,2,1,0:T(8,128)(2,1)} %param.11) | copy-start | bytes 3145732
  4.6 16.6 %copy-start.9 = (bf16[128,32]{0,1:T(8,128)(2,1)S(1)}, bf16[128,32]{0,1:T(8,128)(2,1)}, u32[]{:S(2)}) copy-start(bf16[128,32]{0,1:T(8,128)(2,1)} %param.17) | copy-start | bytes 24580
  4.6 16.8 %copy-start.10 = (bf16[1,128]{1,0:T(2,128)(2,1)S(1)}, bf16[1,128]{1,0:T(2,128)(2,1)}, u32[]{:S(2)}) copy-start(bf16[1,128]{1,0:T(2,128)(2,1)} %param.21) | copy-start | bytes 772
  7.6 35.7 %all-to-all-start = ((bf16[64,48,128]{2,1,0:T(8,128)(2,1)}), bf16[64,48,128]{2,1,0:T(8,128)(2,1)S(1)}, u32[]{:S(2)}, u32[]{:S(2)}) async-start(bf16[64,48,128]{2,1,0:T(8,128)(2,1)} %get-tuple-element.6), calls=%async_computation | async-start | bytes 1572864 | tf_op jit(solution)/shard_map/all_to_all | solution.py:291
  21.5 21.9 %copy-start.2 = (bf16[128,128]{1,0:T(8,128)(2,1)S(1)}, bf16[128,128]{1,0:T(8,128)(2,1)}, u32[]{:S(2)}) copy-start(bf16[128,128]{1,0:T(8,128)(2,1)} %w_mid_ref.1) | copy-start | bytes 98308
  21.5 21.9 %copy-start.3 = (bf16[128,128]{1,0:T(8,128)(2,1)S(1)}, bf16[128,128]{1,0:T(8,128)(2,1)}, u32[]{:S(2)}) copy-start(bf16[128,128]{1,0:T(8,128)(2,1)} %w_last_ref.1) | copy-start | bytes 98308
  21.5 21.9 %copy-start.4 = (bf16[128,128]{1,0:T(8,128)(2,1)S(1)}, bf16[128,128]{1,0:T(8,128)(2,1)}, u32[]{:S(2)}) copy-start(bf16[128,128]{1,0:T(8,128)(2,1)} %w_feat_ref.1) | copy-start | bytes 98308
  118.5 22.6 %all-to-all-start.1 = ((bf16[64,32,128]{2,1,0:T(8,128)(2,1)}), bf16[64,32,128]{2,1,0:T(8,128)(2,1)S(1)}, u32[]{:S(2)}, u32[]{:S(2)}) async-start(bf16[64,32,128]{2,1,0:T(8,128)(2,1)} %get-tuple-element.7), calls=%async_computation.1 | async-start | bytes 1048576 | tf_op jit(solution)/shard_map/all_to_all | solution.py:300
  144.0 13.0 %all-to-all-start.3 = ((bf16[4,48,1024]{2,1,0:T(8,128)(2,1)}), bf16[4,48,1024]{2,1,0:T(8,128)(2,1)S(1)}, u32[]{:S(2)}, u32[]{:S(2)}) async-start(bf16[4,48,1024]{2,1,0:T(8,128)(2,1)} %pad_maximum_fusion.1), calls=%async_computation.3 | async-start | bytes 786432 | tf_op jit(solution)/shard_map/all_to_all | solution.py:321

commit v2 on v1

--- a/solution.py
+++ b/solution.py
@@ -1,5 +1,3 @@
-import functools
-
 import jax
 import jax.numpy as jnp
 from jax import lax
@@ -16,6 +14,7 @@
 CAP = 32
 HALF = CAP // 2
 ROWS = 48
+BACK = CAP + 8
 RAYS = 1024
 SLOTS = COLS * CAP
 TILE = 128
@@ -24,6 +23,7 @@
 WIDE = 256
 F32 = jnp.float32
 BF16 = jnp.bfloat16
+MESH = pl.DeviceIdType.MESH
 
 
 def iota(shape, dim, dtype=jnp.int32):
@@ -42,14 +42,85 @@
     return lax.dot_general(a, b, (((1,), (1,)), ((), ())), preferred_element_type=F32)
 
 
-def ask_kernel(owner_ref, slot_ref, base_ref, weight_ref, spacing_ref, sent_ref, place_ref):
+def greet(barrier, count):
+    me = lax.axis_index("cols")
+
+    def signal(step, carried):
+        peer = lax.rem(me + step, count)
+        pl.semaphore_signal(barrier, inc=1, device_id={"cols": peer}, device_id_type=MESH)
+        return carried
+
+    lax.fori_loop(1, count, signal, 0)
+
+
+def exchange(from_ref, to_ref, send_sem, recv_sem, local_sem):
+    me = lax.axis_index("cols")
+
+    def send(step, carried):
+        peer = lax.rem(me + step, COLS)
+        pltpu.make_async_remote_copy(
+            src_ref=from_ref.at[peer],
+            dst_ref=to_ref.at[me],
+            send_sem=send_sem,
+            recv_sem=recv_sem,
+            device_id={"cols": peer},
+            device_id_type=MESH,
+        ).start()
+        return carried
+
+    lax.fori_loop(1, COLS, send, 0)
+    own = pltpu.make_async_copy(from_ref.at[me], to_ref.at[me], local_sem)
+    own.start()
+    own.wait()
+    others = pl.ds(0, COLS - 1)
+    pltpu.make_async_copy(from_ref.at[others], from_ref.at[others], send_sem).wait()
+    pltpu.make_async_copy(to_ref.at[others], to_ref.at[others], recv_sem).wait()
+
+
+def ask_kernel(
+    owner_hbm,
+    slot_hbm,
+    base_hbm,
+    weight_hbm,
+    spacing_hbm,
+    got_ref,
+    place_ref,
+    sent_ref,
+    owner_ref,
+    slot_ref,
+    base_ref,
+    weight_ref,
+    spacing_ref,
+    load_sem,
+    send_sem,
+    recv_sem,
+    local_sem,
+):
+    loads = [
+        pltpu.make_async_copy(source, target, load_sem.at[i])
+        for i, (source, target) in enumerate(
+            (
+                (owner_hbm, owner_ref),
+                (slot_hbm, slot_ref),
+                (base_hbm, base_ref),
+                (weight_hbm, weight_ref),
+                (spacing_hbm, spacing_ref),
+            )
+        )
+    ]
+    for load in loads:
+        load.start()
+    barrier = pltpu.get_barrier_semaphore()
+    greet(barrier, COLS)
+    for load in loads:
+        load.wait()
     owner = owner_ref[...]
     mine = iota((COLS, RAYS), 0) == owner
     earlier = one_hot(iota((RAYS, RAYS), 0) < iota((RAYS, RAYS), 1))
     count = dot(one_hot(mine), earlier)
     rank = jnp.sum(jnp.where(mine, count, 0.0), axis=0, keepdims=True).astype(jnp.int32)
     place = owner * CAP + rank
-    place_ref[...] = place
+    place_ref[...] = jnp.concatenate([owner, rank], axis=0)
     sent = dot_rows(one_hot(iota((SLOTS, RAYS), 0) == place), weight_ref[...])
     sent_ref[:, :CAP, :] = sent.astype(BF16).reshape(COLS, CAP, HID)
     base = base_ref[...].astype(F32) + 0.5
@@ -69,6 +140,8 @@
     row = owner * HALF + jnp.where(second, rank - HALF, rank)
     sent = dot_rows(one_hot(iota((COLS * HALF, RAYS), 0) == row), both)
     sent_ref[:, CAP:, :] = sent.astype(BF16).reshape(COLS, HALF, HID)
+    pl.semaphore_wait(barrier, COLS - 1)
+    exchange(sent_ref, got_ref, send_sem, recv_sem, local_sem)
 
 
 def field_kernel(
@@ -79,8 +152,7 @@
     w_last_ref,
     w_feat_ref,
     w_density_ref,
-    colour_ref,
-    depth_ref,
+    block_ref,
     table_ref,
     pos_ref,
     weight_ref,
@@ -210,17 +282,109 @@
     lax.fori_loop(0, tile_count, one_tile, 0)
     for part in range(2):
         block = reply_ref[:HID, part * half : (part + 1) * half].T
-        colour_ref[:, part * HALF : (part + 1) * HALF, :] = block.astype(BF16).reshape(
+        block_ref[:, part * HALF : (part + 1) * HALF, :] = block.astype(BF16).reshape(
             COLS, HALF, HID
         )
-    depth_ref[...] = reply_ref[HID : HID + 16, :].astype(BF16)
-
-
-def collect_kernel(colour_ref, depth_ref, place_ref, out_ref):
-    table = colour_ref[...].reshape(SLOTS, HID).astype(F32).T.astype(BF16)
-    found = one_hot(iota((SLOTS, RAYS), 0) == place_ref[...])
-    out_ref[:HID, :] = dot(table, found).astype(BF16)
-    out_ref[HID:, :] = dot(depth_ref[...], found).astype(BF16)
+    index = iota((1, SLOTS), 1, F32)
+    part = jnp.floor(index * (1.0 / half))
+    inside = index - part * half
+    column = jnp.floor(inside * (1.0 / HALF))
+    rank = inside - column * HALF + part * HALF
+    columns = one_hot(iota((COLS, SLOTS), 0, F32) == column)
+    ranks = iota((CAP, SLOTS), 0, F32) == rank
+    spots = jnp.concatenate(
+        [jnp.where(ranks, reply_ref[HID + i : HID + i + 1, :], 0.0) for i in range(4)], axis=0
+    ).astype(BF16)
+    depth = dot_rows(columns, spots)
+    block_ref[:, CAP:, :] = jnp.broadcast_to(depth.reshape(COLS, 1, HID), (COLS, 8, HID)).astype(BF16)
+
+
+def collect_kernel(
+    block_ref,
+    place_ref,
+    image_ref,
+    visible_ref,
+    got_ref,
+    here_ref,
+    thick_ref,
+    colours_ref,
+    thicks_ref,
+    send_sem,
+    recv_sem,
+    local_sem,
+    colour_send,
+    colour_recv,
+    thick_send,
+    thick_recv,
+):
+    regions = lax.axis_size("depth")
+    me = lax.axis_index("depth")
+    barrier = pltpu.get_barrier_semaphore()
+    greet(barrier, COLS)
+    for step in range(1, regions):
+        peer = lax.rem(me + step, regions)
+        pl.semaphore_signal(barrier, inc=1, device_id={"depth": peer}, device_id_type=MESH)
+    owner = place_ref[0:1, :]
+    rank = place_ref[1:2, :]
+    pl.semaphore_wait(barrier, COLS - 1 + regions - 1)
+    exchange(block_ref, got_ref, send_sem, recv_sem, local_sem)
+    mine = one_hot(iota((COLS, RAYS), 0) == owner)
+    depth = jnp.max(got_ref[:, CAP:, :].astype(F32), axis=1)
+    depth = dot(depth.T.astype(BF16), mine)
+    ranks = iota((CAP, RAYS), 0) == rank
+    thick = jnp.zeros((1, RAYS), F32)
+    for i in range(3):
+        piece = jnp.where(ranks, depth[i * CAP : (i + 1) * CAP], 0.0)
+        thick = thick + jnp.sum(piece, axis=0, keepdims=True)
+    thick_ref[...] = thick
+    copies = []
+    for step in range(1, regions):
+        peer = lax.rem(me + step, regions)
+        copy = pltpu.make_async_remote_copy(
+            src_ref=thick_ref,
+            dst_ref=thicks_ref.at[step],
+            send_sem=thick_send.at[step],
+            recv_sem=thick_recv.at[step],
+            device_id={"depth": peer},
+            device_id_type=MESH,
+        )
+        copy.start()
+        copies.append(copy)
+    table = got_ref[:, :CAP, :].reshape(SLOTS, HID).astype(F32).T.astype(BF16)
+    found = one_hot(iota((SLOTS, RAYS), 0) == owner * CAP + rank)
+    rows = HID // regions
+    here_ref[...] = dot(table, found).astype(BF16).reshape(regions, rows, RAYS)
+    for step in range(1, regions):
+        peer = lax.rem(me + step, regions)
+        copy = pltpu.make_async_remote_copy(
+            src_ref=here_ref.at[peer],
+            dst_ref=colours_ref.at[step],
+            send_sem=colour_send.at[step],
+            recv_sem=colour_recv.at[step],
+            device_id={"depth": peer},
+            device_id_type=MESH,
+        )
+        copy.start()
+        copies.append(copy)
+    for copy in copies:
+        copy.wait()
+    parts = [thick] + [thicks_ref[step] for step in range(1, regions)]
+    sources = [lax.rem(me - step + regions, regions) for step in range(regions)]
+    image = jnp.zeros((rows, RAYS), F32)
+    for step in range(regions):
+        ahead = jnp.zeros((1, RAYS), F32)
+        for other in range(regions):
+            if other != step:
+                front = (sources[other] < sources[step]).astype(F32)
+                ahead = ahead + front * parts[other]
+        visible = jnp.exp(-ahead)
+        if step == 0:
+            visible_ref[...] = visible
+            colour = here_ref[me]
+        else:
+            colour = colours_ref[step]
+        image = image + visible * colour.astype(F32)
+    image_ref[...] = image
 
 
 def vmem(count):
@@ -235,12 +399,9 @@
 def run_field(got, table, w_in, w_mid, w_last, w_feat, w_density):
     return pl.pallas_call(
         field_kernel,
-        out_shape=(
-            jax.ShapeDtypeStruct((COLS, CAP, HID), BF16),
-            jax.ShapeDtypeStruct((16, SLOTS), BF16),
-        ),
+        out_shape=jax.ShapeDtypeStruct((COLS, BACK, HID), BF16),
         in_specs=vmem(7),
-        out_specs=tuple(vmem(2)),
+        out_specs=vmem(1)[0],
         scratch_shapes=[
             pltpu.VMEM((SLOTS, 2 * HID), BF16),
             pltpu.VMEM((8, SLOTS), F32),
@@ -270,16 +431,29 @@
     w_feat,
     w_density,
 ):
-    params = pltpu.CompilerParams(vmem_limit_bytes=48 << 20)
-    sent, place = pl.pallas_call(
+    got, place = pl.pallas_call(
         ask_kernel,
         out_shape=(
             jax.ShapeDtypeStruct((COLS, ROWS, HID), BF16),
-            jax.ShapeDtypeStruct((1, RAYS), jnp.int32),
+            jax.ShapeDtypeStruct((2, RAYS), jnp.int32),
         ),
-        in_specs=vmem(5),
+        in_specs=[pl.BlockSpec(memory_space=pl.ANY)] * 5,
         out_specs=tuple(vmem(2)),
-        compiler_params=params,
+        scratch_shapes=[
+            pltpu.VMEM((COLS, ROWS, HID), BF16),
+            pltpu.VMEM((1, RAYS), jnp.int32),
+            pltpu.VMEM((1, RAYS), jnp.int32),
+            pltpu.VMEM((S, RAYS), jnp.int32),
+            pltpu.VMEM((HID, RAYS), BF16),
+            pltpu.VMEM((S, RAYS), BF16),
+            pltpu.SemaphoreType.DMA((5,)),
+            pltpu.SemaphoreType.DMA,
+            pltpu.SemaphoreType.DMA,
+            pltpu.SemaphoreType.DMA,
+        ],
+        compiler_params=pltpu.CompilerParams(
+            vmem_limit_bytes=32 << 20, collective_id=0, has_side_effects=True
+        ),
         name="ask",
     )(
         brick_owner.reshape(1, RAYS),
@@ -288,48 +462,37 @@
         corner_weights[0].reshape(HID, RAYS),
         spacing[0],
     )
-    got = lax.all_to_all(sent, "cols", split_axis=0, concat_axis=0, tiled=True)
     table = make_table(bricks[0])
-    colour, depth = run_field(got, table, w_in, w_mid, w_last, w_feat, w_density)
-    return colour, depth, place
-
-
-def finish(colour, depth, place):
-    params = pltpu.CompilerParams(vmem_limit_bytes=48 << 20)
-    depth = depth[:3].reshape(3, 2, COLS, HALF).transpose(2, 0, 1, 3).reshape(COLS, 3 * CAP)
-    colour = lax.all_to_all(colour, "cols", split_axis=0, concat_axis=0, tiled=True)
-    depth = lax.all_to_all(depth, "cols", split_axis=0, concat_axis=0, tiled=True)
-    depth = depth.reshape(COLS, 3, CAP).transpose(1, 0, 2).reshape(3, SLOTS)
-    depth = jnp.pad(depth, ((0, 13), (0, 0)))
-    here = pl.pallas_call(
-        collect_kernel,
-        out_shape=jax.ShapeDtypeStruct((HID + 16, RAYS), BF16),
-        in_specs=vmem(3),
-        out_specs=vmem(1)[0],
-        compiler_params=params,
-        name="collect",
-    )(colour, depth, place)
+    block = run_field(got, table, w_in, w_mid, w_last, w_feat, w_density)
     regions = lax.axis_size("depth")
     rows = HID // regions
-    out = jnp.concatenate(
-        [
-            here[:HID].reshape(regions, rows, RAYS),
-            jnp.broadcast_to(here[HID:][None], (regions, 16, RAYS)),
+    return pl.pallas_call(
+        collect_kernel,
+        out_shape=(
+            jax.ShapeDtypeStruct((rows, RAYS), F32),
+            jax.ShapeDtypeStruct((1, RAYS), F32),
+        ),
+        in_specs=vmem(2),
+        out_specs=tuple(vmem(2)),
+        scratch_shapes=[
+            pltpu.VMEM((COLS, BACK, HID), BF16),
+            pltpu.VMEM((regions, rows, RAYS), BF16),
+            pltpu.VMEM((1, RAYS), F32),
+            pltpu.VMEM((regions, rows, RAYS), BF16),
+            pltpu.VMEM((regions, 1, RAYS), F32),
+            pltpu.SemaphoreType.DMA,
+            pltpu.SemaphoreType.DMA,
+            pltpu.SemaphoreType.DMA,
+            pltpu.SemaphoreType.DMA((regions,)),
+            pltpu.SemaphoreType.DMA((regions,)),
+            pltpu.SemaphoreType.DMA((regions,)),
+            pltpu.SemaphoreType.DMA((regions,)),
         ],
-        axis=1,
-    )
-    out = lax.all_to_all(out, "depth", split_axis=0, concat_axis=0, tiled=True)
-    thick = jnp.sum(out[:, rows : rows + 3].astype(F32), axis=1)
-    ahead = jnp.cumsum(thick, axis=0) - thick
-    visible = jnp.exp(-ahead)
-    image = jnp.sum(visible[:, None, :] * out[:, :rows].astype(F32), axis=0)
-    me = lax.axis_index("depth")
-    mine = jnp.sum(jnp.where(jnp.arange(regions)[:, None] == me, visible, 0.0), axis=0)
-    return image, mine[None, :]
-
-
-def whole(*args):
-    return finish(*on_device(*args))
+        compiler_params=pltpu.CompilerParams(
+            vmem_limit_bytes=32 << 20, collective_id=1, has_side_effects=True
+        ),
+        name="collect",
+    )(block, place)
 
 
 def solution(mesh):
@@ -348,5 +511,5 @@
     )
     out_specs = (P("depth", "cols"), P("depth", "cols"))
     return jax.shard_map(
-        whole, mesh=mesh, in_specs=in_specs, out_specs=out_specs, check_vma=False
+        on_device, mesh=mesh, in_specs=in_specs, out_specs=out_specs, check_vma=False
     )

time: 159 us -> 126 us (0.79)
  Pallas kernels: 58.8 us -> 121 us
  waiting for transfers between devices: 46.4 us -> 0 us
  starting transfers between devices: 23.5 us -> 0 us
  blocking collectives: 21.1 us -> 0 us
  other arithmetic: 2.4 us -> 0.16 us
  local copies, waits for them, and re-layouts: 5.43 us -> 3.72 us
    all_to_all x3 -> x0, waiting for transfers between devices: 46.4 us -> none  [the longest x1 21.7 us: on_device(): got = lax.all_to_all(sent, 'cols', split_axis=0, concat_axis=0, tiled=True)]
    pallas_call x2, Pallas kernels: 55.8 us -> 91.5 us  [the longest x1 64.6 us: on_device(): pl.pallas_call(collect_kernel, out_shape=(jax.ShapeDtypeStruct((rows, RAY...]
    pallas_call x1, Pallas kernels: 3.08 us -> 30 us  [on_device(): pl.pallas_call(ask_kernel, out_shape=(jax.ShapeDtypeStruct((COLS, ROWS, H...]
    all_to_all x3 -> x0, starting transfers between devices: 23.5 us -> none  [the longest x1 13 us: on_device(): got = lax.all_to_all(sent, 'cols', split_axis=0, concat_axis=0, tiled=True)]
    all_to_all x1 -> x0, blocking collectives: 21.1 us -> none  [finish(): lax.all_to_all(depth, 'cols', split_axis=0, concat_axis=0, tiled=True)]
  transfers between devices with their start and end apart: 3 -> 0, of which waited for: 3 -> 0; matrix products, arithmetic and copies ran while one was open for 1% -> 0% of each run, Pallas kernels for 0% -> 0%
where the time goes in v2:
time: 126 us
  Pallas kernels  121 us (96%)
  local copies, waits for them, and re-layouts  3.72 us (3%)
    pallas_call x1, Pallas kernels, on_device(): pl.pallas_call(collect_kernel, out_shape=(jax.ShapeDtypeStruct((rows, RAY...  64.6 us
    pallas_call x1, Pallas kernels, on_device(): pl.pallas_call(ask_kernel, out_shape=(jax.ShapeDtypeStruct((COLS, ROWS, H...  30 us
    pallas_call x1, Pallas kernels, run_field(): pl.pallas_call(field_kernel, out_shape=jax.ShapeDtypeStruct((COLS, BACK,...  26.9 us
    unnamed x24, local copies, waits for them, and re-layouts  3.58 us

profile of v2, /device:TPU:1, one launch (start us, length us, event | category | flops | bytes accessed | tf_op | source)
XLA Modules:
  0.0 126.1 jit_solution(15072415166672158669)
XLA Ops:
  0.6 1.5 %copy.13 = bf16[1,4,256,512]{2,3,1,0:T(8,128)(2,1)S(1)} copy(bf16[1,4,256,512]{3,2,1,0:T(8,128)(2,1)} %param.11) | data formatting | bytes 2097152 | tf_op args[0]
  2.1 0.1 fusion
  2.3 0.0 copy-start
  2.3 0.0 copy-start.1
  2.3 0.0 copy-start.5
  2.3 0.0 copy-start.6
  2.3 0.0 copy-start.7
  2.3 0.0 copy-start.8
  2.3 0.0 copy-start.9
  2.3 0.0 copy-start.2
  2.4 0.0 copy-start.3
  2.4 0.0 copy-start.4
  2.4 0.2 pad_maximum_fusion.brick_ref
  2.5 0.7 copy-done
  3.2 0.0 copy-done.1
  3.2 0.0 copy-done.5
  3.2 0.0 copy-done.6
  3.2 0.0 copy-done.7
  3.2 30.0 %ask.1 = (bf16[64,48,128]{2,1,0:T(8,128)(2,1)S(1)}, s32[2,1024]{1,0:T(2,128)S(1)}) custom-call(s32[1,1024]{1,0:T(1,128)S(1)} %bitcast.10, s32[1,1024]{1,0:T(1,128)S(1)} %copy-done.7, s32[16,1024]{1,0:T(8,128)S(1)} %bitcast.8, bf16[128,1024]{1,0:T(8,128)(2,1)S(1)} %bitcast.7, bf16[16,1024]{1,0:T(8,128)(2,1)S(1)} %bitcast.9), custom_call_target="tpu_custom_call" | custom-call | tf_op jit(solution)/shard_map/ask/pallas_call | solution.py:434
  33.2 0.0 copy-done.8
  33.2 0.1 copy.14.w_in_ref
  33.3 0.0 copy-done.9
  33.3 0.0 copy-done.2
  33.3 0.0 copy-done.3
  33.4 0.0 copy-done.4
  33.4 26.9 %field.1.block_ref = bf16[64,40,128]{2,1,0:T(8,128)(2,1)S(1)} custom-call(bf16[64,48,128]{2,1,0:T(8,128)(2,1)S(1)} %get-tuple-element.4.got_ref, bf16[4,480,512]{2,1,0:T(8,128)(2,1)S(1)} %pad_maximum_fusion.brick_ref, bf16[128,32]{1,0:T(8,128)(2,1)S(1)} %copy.14.w_in_ref, bf16[128,128]{1,0:T(8,128)(2,1)S(1)} %copy-done.2, bf16[128,128]{1,0:T(8,128)(2,1)S(1)} %copy-done.3, ...), custom_call_target="tpu_custom_call" | custom-call | tf_op jit(solution)/shard_map/field/pallas_call | solution.py:400
  60.3 64.6 %collect.1 = (f32[32,1024]{1,0:T(8,128)S(1)}, f32[1,1024]{1,0:T(1,128)S(1)}) custom-call(bf16[64,40,128]{2,1,0:T(8,128)(2,1)S(1)} %field.1.block_ref, s32[2,1024]{1,0:T(2,128)S(1)} %get-tuple-element.5.place_ref), custom_call_target="tpu_custom_call" | custom-call | tf_op jit(solution)/shard_map/collect/pallas_call | solution.py:469
  124.8 0.7 copy.17
  125.5 0.6 copy.18
  (1 shorter events, 0.0 us)
Async XLA Ops:
  2.3 1.0 copy-start
  2.3 0.9 copy-start.1
  2.3 0.9 copy-start.5
  2.3 0.9 copy-start.6
  2.3 0.9 copy-start.7
  2.3 30.9 %copy-start.8 = (bf16[128,32]{0,1:T(8,128)(2,1)S(1)}, bf16[128,32]{0,1:T(8,128)(2,1)}, u32[]{:S(2)}) copy-start(bf16[128,32]{0,1:T(8,128)(2,1)} %param.17) | copy-start | bytes 24580
  2.3 31.0 %copy-start.9 = (bf16[1,128]{1,0:T(2,128)(2,1)S(1)}, bf16[1,128]{1,0:T(2,128)(2,1)}, u32[]{:S(2)}) copy-start(bf16[1,128]{1,0:T(2,128)(2,1)} %param.21) | copy-start | bytes 772
  2.3 31.0 %copy-start.2 = (bf16[128,128]{1,0:T(8,128)(2,1)S(1)}, bf16[128,128]{1,0:T(8,128)(2,1)}, u32[]{:S(2)}) copy-start(bf16[128,128]{1,0:T(8,128)(2,1)} %w_mid_ref.1) | copy-start | bytes 98308
  2.4 31.0 %copy-start.3 = (bf16[128,128]{1,0:T(8,128)(2,1)S(1)}, bf16[128,128]{1,0:T(8,128)(2,1)}, u32[]{:S(2)}) copy-start(bf16[128,128]{1,0:T(8,128)(2,1)} %w_last_ref.1) | copy-start | bytes 98308
  2.4 31.0 %copy-start.4 = (bf16[128,128]{1,0:T(8,128)(2,1)S(1)}, bf16[128,128]{1,0:T(8,128)(2,1)}, u32[]{:S(2)}) copy-start(bf16[128,128]{1,0:T(8,128)(2,1)} %w_feat_ref.1) | copy-start | bytes 98308

commit v3 on v2

--- a/solution.py
+++ b/solution.py
@@ -14,13 +14,16 @@
 CAP = 32
 HALF = CAP // 2
 ROWS = 48
-BACK = CAP + 8
 RAYS = 1024
 SLOTS = COLS * CAP
 TILE = 128
 MAX_TILES = SLOTS // TILE + 3
 POS = EDGE - 1
 WIDE = 256
+EACH = WIDE // TILE
+GATHER = 4
+SPACE = MAX_TILES + 1
+BUFFERS = 2
 F32 = jnp.float32
 BF16 = jnp.bfloat16
 MESH = pl.DeviceIdType.MESH
@@ -53,7 +56,7 @@
     lax.fori_loop(1, count, signal, 0)
 
 
-def exchange(from_ref, to_ref, send_sem, recv_sem, local_sem):
+def start_exchange(from_ref, to_ref, send_sem, recv_sem, local_sem):
     me = lax.axis_index("cols")
 
     def send(step, carried):
@@ -69,10 +72,13 @@
         return carried
 
     lax.fori_loop(1, COLS, send, 0)
-    own = pltpu.make_async_copy(from_ref.at[me], to_ref.at[me], local_sem)
-    own.start()
-    own.wait()
+    pltpu.make_async_copy(from_ref.at[me], to_ref.at[me], local_sem).start()
+
+
+def end_exchange(from_ref, to_ref, send_sem, recv_sem, local_sem):
+    me = lax.axis_index("cols")
     others = pl.ds(0, COLS - 1)
+    pltpu.make_async_copy(from_ref.at[me], to_ref.at[me], local_sem).wait()
     pltpu.make_async_copy(from_ref.at[others], from_ref.at[others], send_sem).wait()
     pltpu.make_async_copy(to_ref.at[others], to_ref.at[others], recv_sem).wait()
 
@@ -83,15 +89,20 @@
     base_hbm,
     weight_hbm,
     spacing_hbm,
+    brick_hbm,
     got_ref,
     place_ref,
+    table_hbm,
     sent_ref,
     owner_ref,
     slot_ref,
     base_ref,
     weight_ref,
     spacing_ref,
+    brick_ref,
+    table_ref,
     load_sem,
+    table_sem,
     send_sem,
     recv_sem,
     local_sem,
@@ -105,6 +116,7 @@
                 (base_hbm, base_ref),
                 (weight_hbm, weight_ref),
                 (spacing_hbm, spacing_ref),
+                (brick_hbm, brick_ref),
             )
         )
     ]
@@ -112,7 +124,7 @@
         load.start()
     barrier = pltpu.get_barrier_semaphore()
     greet(barrier, COLS)
-    for load in loads:
+    for load in loads[:5]:
         load.wait()
     owner = owner_ref[...]
     mine = iota((COLS, RAYS), 0) == owner
@@ -141,28 +153,67 @@
     sent = dot_rows(one_hot(iota((COLS * HALF, RAYS), 0) == row), both)
     sent_ref[:, CAP:, :] = sent.astype(BF16).reshape(COLS, HALF, HID)
     pl.semaphore_wait(barrier, COLS - 1)
-    exchange(sent_ref, got_ref, send_sem, recv_sem, local_sem)
+    start_exchange(sent_ref, got_ref, send_sem, recv_sem, local_sem)
+    loads[5].wait()
+    for q in range(brick_ref.shape[0]):
+        turned = brick_ref[q].astype(F32).T.astype(BF16)
+        table_ref[q, :, :LINES] = turned[: POS * CH]
+        table_ref[q, :, LINES:] = turned[CH:]
+    store = pltpu.make_async_copy(table_ref, table_hbm, table_sem)
+    store.start()
+    store.wait()
+    end_exchange(sent_ref, got_ref, send_sem, recv_sem, local_sem)
 
 
 def field_kernel(
+    got_hbm,
+    brick_hbm,
+    w_in_hbm,
+    w_mid_hbm,
+    w_last_hbm,
+    w_feat_hbm,
+    w_density_hbm,
+    colour_ref,
+    depth_ref,
     got_ref,
     brick_ref,
+    turned_ref,
     w_in_ref,
     w_mid_ref,
     w_last_ref,
     w_feat_ref,
+    thin_ref,
     w_density_ref,
-    block_ref,
+    load_sem,
     table_ref,
     pos_ref,
+    chosen_ref,
     weight_ref,
     feature_ref,
     mix_ref,
     mixed_ref,
     hidden_ref,
     density_ref,
+    result_ref,
     reply_ref,
 ):
+    loads = [
+        pltpu.make_async_copy(source, target, load_sem.at[i])
+        for i, (source, target) in enumerate(
+            (
+                (got_hbm, got_ref),
+                (brick_hbm, brick_ref),
+                (w_in_hbm, turned_ref),
+                (w_mid_hbm, w_mid_ref),
+                (w_last_hbm, w_last_ref),
+                (w_feat_hbm, w_feat_ref),
+                (w_density_hbm, thin_ref),
+            )
+        )
+    ]
+    for load in loads:
+        load.start()
+    loads[0].wait()
     half = COLS * HALF
     second = got_ref[:, CAP:, :].reshape(half, HID)
     lane = iota((half, HID), 1)
@@ -199,63 +250,75 @@
     pos_ref[...] = jnp.broadcast_to(pos, (8, SLOTS))
     limit1, limit2, limit3, tile_count = [start.astype(jnp.int32) for start in starts]
     reply_ref[...] = jnp.zeros_like(reply_ref)
-
-    def one_tile(tile, carried):
+    result_ref[...] = jnp.zeros_like(result_ref)
+
+    def gather(step, carried):
+        for u in range(GATHER):
+            tile = step * GATHER + u
+            local = pos_ref[0:1, :] - (tile * TILE).astype(F32)
+            chosen_ref[tile] = one_hot(iota((TILE, SLOTS), 0, F32) == local)
+        chosen = chosen_ref[pl.ds(step * GATHER, GATHER)].reshape(GATHER * TILE, SLOTS)
+        rays = dot(chosen, table_ref[...])
+        for u in range(GATHER):
+            turned = rays[u * TILE : (u + 1) * TILE].T
+            weight_ref[step * GATHER + u] = turned[:HID]
+            feature_ref[step * GATHER + u] = turned[HID : HID + HID // 2] + turned[HID + HID // 2 :]
+        return carried
+
+    lax.fori_loop(0, lax.div(tile_count + GATHER - 1, GATHER), gather, 0)
+
+    def build(tile, u, s):
+        lanes = slice(s * TILE, (s + 1) * TILE)
+        line = feature_ref[tile, s : s + 1, :]
+        coord_x = jnp.floor(line * (1.0 / EDGE))
+        coord_y = line - coord_x * EDGE
+        rows = iota((EDGE, TILE), 0, F32)
+        near = rows == coord_y
+        far = rows == coord_y + 1.0
+        x_full = jnp.broadcast_to(coord_x, (EDGE, TILE)).astype(BF16)
+        none = jnp.zeros((EDGE, TILE), BF16)
+        for e in range(2):
+            parts = []
+            for a in range(2):
+                low = weight_ref[tile, (4 * a + e) * S + s : (4 * a + e) * S + s + 1, :]
+                high = weight_ref[tile, (4 * a + 2 + e) * S + s : (4 * a + 2 + e) * S + s + 1, :]
+                parts.append(jnp.where(near, low, jnp.where(far, high, 0.0)).astype(BF16))
+            for x in range(EDGE):
+                value = jnp.where(x_full == x, parts[0], none)
+                if x > 0:
+                    value = jnp.where(x_full == x - 1, parts[1], value)
+                mix_ref[u, e * LINES + x * EDGE : e * LINES + (x + 1) * EDGE, lanes] = value
+
+    def spread(tile, u, group):
         brick = (
             (tile >= limit1).astype(jnp.int32)
             + (tile >= limit2).astype(jnp.int32)
             + (tile >= limit3).astype(jnp.int32)
         )
-        local = pos_ref[0:1, :] - (tile * TILE).astype(F32)
-        chosen = one_hot(iota((TILE, SLOTS), 0, F32) == local)
-        rays = dot(chosen, table_ref[...]).T
-        weight_ref[...] = rays[:HID]
-        feature_ref[...] = rays[HID : HID + HID // 2] + rays[HID + HID // 2 :]
-
-        for s in range(S):
-            lanes = slice(s * TILE, (s + 1) * TILE)
-            line = feature_ref[s : s + 1, :]
-            coord_x = jnp.floor(line * (1.0 / EDGE))
-            coord_y = line - coord_x * EDGE
-            rows = iota((EDGE, TILE), 0, F32)
-            near = rows == coord_y
-            far = rows == coord_y + 1.0
-            x_full = jnp.broadcast_to(coord_x, (EDGE, TILE)).astype(BF16)
-            none = jnp.zeros((EDGE, TILE), BF16)
-            for e in range(2):
-                parts = []
-                for a in range(2):
-                    low = weight_ref[(4 * a + e) * S + s : (4 * a + e) * S + s + 1, :]
-                    high = weight_ref[(4 * a + 2 + e) * S + s : (4 * a + 2 + e) * S + s + 1, :]
-                    parts.append(jnp.where(near, low, jnp.where(far, high, 0.0)).astype(BF16))
-                for x in range(EDGE):
-                    value = jnp.where(x_full == x, parts[0], none)
-                    if x > 0:
-                        value = jnp.where(x_full == x - 1, parts[1], value)
-                    mix_ref[e * LINES + x * EDGE : e * LINES + (x + 1) * EDGE, lanes] = value
-        for group in range(S * TILE // WIDE):
-            lanes = slice(group * WIDE, (group + 1) * WIDE)
-            spread = dot(brick_ref[brick], mix_ref[:, lanes])
-            each = WIDE // TILE
-            coord_z = jnp.concatenate(
-                [feature_ref[S + each * group + i : S + each * group + i + 1, :] for i in range(each)],
-                axis=1,
-            )
-            mixed = jnp.zeros((CH, WIDE), F32)
-            for p in range(POS):
-                mixed = jnp.where(coord_z == float(p), spread[p * CH : (p + 1) * CH], mixed)
-            mixed_ref[:, lanes] = mixed.astype(BF16)
-        layer = mixed_ref[...]
+        lanes = slice(group * WIDE, (group + 1) * WIDE)
+        read = dot(brick_ref[brick], mix_ref[u, :, lanes])
+        coord_z = jnp.concatenate(
+            [feature_ref[tile, S + EACH * group + i : S + EACH * group + i + 1, :] for i in range(EACH)],
+            axis=1,
+        )
+        mixed = jnp.zeros((CH, WIDE), F32)
+        for p in range(POS):
+            mixed = jnp.where(coord_z == float(p), read[p * CH : (p + 1) * CH], mixed)
+        mixed_ref[u, :, lanes] = mixed.astype(BF16)
+
+    def shade(u):
+        layer = mixed_ref[u]
         for w_ref in (w_in_ref, w_mid_ref, w_last_ref):
             layer = jnp.maximum(dot(w_ref[...], layer), 0.0).astype(BF16)
-        hidden_ref[...] = layer
+        hidden_ref[u] = layer
         thin = dot(w_density_ref[...], layer)
         for s in range(S):
-            density_ref[s : s + 1, :] = thin[0:1, s * TILE : (s + 1) * TILE]
-
-        density = density_ref[...]
+            density_ref[u, s : s + 1, :] = thin[0:1, s * TILE : (s + 1) * TILE]
+
+    def composite(tile, u):
+        density = density_ref[u]
         density = jnp.maximum(density, 0.0) + jnp.log1p(jnp.exp(-jnp.abs(density)))
-        optical = density * feature_ref[2 * S : 3 * S, :]
+        optical = density * feature_ref[tile, 2 * S : 3 * S, :]
         ahead = [jnp.zeros((1, TILE), F32)]
         for s in range(S):
             ahead.append(ahead[s] + optical[s : s + 1])
@@ -263,7 +326,7 @@
         share = clear * (1.0 - jnp.exp(-optical))
         total = jnp.zeros((HID, TILE), F32)
         for s in range(S):
-            hidden = hidden_ref[:, s * TILE : (s + 1) * TILE].astype(F32)
+            hidden = hidden_ref[u, :, s * TILE : (s + 1) * TILE].astype(F32)
             total = total + hidden * share[s : s + 1]
         high = total.astype(BF16)
         low = (total - high.astype(F32)).astype(BF16)
@@ -275,14 +338,47 @@
         extra = jnp.concatenate(
             [thick_high, thick_mid, thick_low, jnp.zeros((13, TILE), F32)], axis=0
         )
-        result = jnp.concatenate([colour, extra], axis=0).astype(BF16)
+        result_ref[tile] = jnp.concatenate([colour, extra], axis=0).astype(BF16)
+
+    for load in loads[1:]:
+        load.wait()
+    w_in_ref[...] = turned_ref[...].astype(F32).T.astype(BF16)
+    w_density_ref[...] = jnp.broadcast_to(thin_ref[...].astype(F32), (16, HID)).astype(BF16)
+    groups = S // EACH
+    for s in range(S):
+        build(0, 0, s)
+
+    def two_tiles(step, carried):
+        tile = 2 * step
+        following = jnp.minimum(tile + 2, SPACE - 1)
+        for group in range(groups):
+            spread(tile, 0, group)
+            for s in range(EACH):
+                build(tile + 1, 1, group * EACH + s)
+        shade(0)
+        for group in range(groups):
+            spread(tile + 1, 1, group)
+            for s in range(EACH):
+                build(following, 0, group * EACH + s)
+            if group == groups // 2:
+                composite(tile, 0)
+        shade(1)
+        composite(tile + 1, 1)
+        return carried
+
+    lax.fori_loop(0, lax.div(tile_count + 1, 2), two_tiles, 0)
+
+    def scatter(step, carried):
+        tiles = [step * GATHER + u for u in range(GATHER)]
+        result = jnp.concatenate([result_ref[tile] for tile in tiles], axis=1)
+        chosen = chosen_ref[pl.ds(step * GATHER, GATHER)].reshape(GATHER * TILE, SLOTS)
         reply_ref[...] += dot(result, chosen)
         return carried
 
-    lax.fori_loop(0, tile_count, one_tile, 0)
+    lax.fori_loop(0, lax.div(tile_count + GATHER - 1, GATHER), scatter, 0)
     for part in range(2):
         block = reply_ref[:HID, part * half : (part + 1) * half].T
-        block_ref[:, part * HALF : (part + 1) * HALF, :] = block.astype(BF16).reshape(
+        colour_ref[:, part * HALF : (part + 1) * HALF, :] = block.astype(BF16).reshape(
             COLS, HALF, HID
         )
     index = iota((1, SLOTS), 1, F32)
@@ -296,15 +392,17 @@
         [jnp.where(ranks, reply_ref[HID + i : HID + i + 1, :], 0.0) for i in range(4)], axis=0
     ).astype(BF16)
     depth = dot_rows(columns, spots)
-    block_ref[:, CAP:, :] = jnp.broadcast_to(depth.reshape(COLS, 1, HID), (COLS, 8, HID)).astype(BF16)
+    depth_ref[...] = depth.reshape(COLS, 1, HID)
 
 
 def collect_kernel(
-    block_ref,
+    colour_ref,
+    depth_ref,
     place_ref,
     image_ref,
     visible_ref,
     got_ref,
+    deep_ref,
     here_ref,
     thick_ref,
     colours_ref,
@@ -312,6 +410,9 @@
     send_sem,
     recv_sem,
     local_sem,
+    deep_send,
+    deep_recv,
+    deep_local,
     colour_send,
     colour_recv,
     thick_send,
@@ -327,9 +428,12 @@
     owner = place_ref[0:1, :]
     rank = place_ref[1:2, :]
     pl.semaphore_wait(barrier, COLS - 1 + regions - 1)
-    exchange(block_ref, got_ref, send_sem, recv_sem, local_sem)
+    start_exchange(depth_ref, deep_ref, deep_send, deep_recv, deep_local)
+    start_exchange(colour_ref, got_ref, send_sem, recv_sem, local_sem)
+    found = one_hot(iota((SLOTS, RAYS), 0) == owner * CAP + rank)
+    end_exchange(depth_ref, deep_ref, deep_send, deep_recv, deep_local)
     mine = one_hot(iota((COLS, RAYS), 0) == owner)
-    depth = jnp.max(got_ref[:, CAP:, :].astype(F32), axis=1)
+    depth = deep_ref[...].reshape(COLS, HID)
     depth = dot(depth.T.astype(BF16), mine)
     ranks = iota((CAP, RAYS), 0) == rank
     thick = jnp.zeros((1, RAYS), F32)
@@ -350,8 +454,8 @@
         )
         copy.start()
         copies.append(copy)
-    table = got_ref[:, :CAP, :].reshape(SLOTS, HID).astype(F32).T.astype(BF16)
-    found = one_hot(iota((SLOTS, RAYS), 0) == owner * CAP + rank)
+    end_exchange(colour_ref, got_ref, send_sem, recv_sem, local_sem)
+    table = got_ref[...].reshape(SLOTS, HID).astype(F32).T.astype(BF16)
     rows = HID // regions
     here_ref[...] = dot(table, found).astype(BF16).reshape(regions, rows, RAYS)
     for step in range(1, regions):
@@ -387,35 +491,49 @@
     image_ref[...] = image
 
 
+def hbm(count):
+    return [pl.BlockSpec(memory_space=pltpu.HBM)] * count
+
+
 def vmem(count):
     return [pl.BlockSpec(memory_space=pltpu.VMEM)] * count
-
-
-def make_table(bricks):
-    turned = jnp.transpose(bricks, (0, 2, 1))
-    return jnp.concatenate([turned[:, : POS * CH], turned[:, CH:]], axis=2)
 
 
 def run_field(got, table, w_in, w_mid, w_last, w_feat, w_density):
     return pl.pallas_call(
         field_kernel,
-        out_shape=jax.ShapeDtypeStruct((COLS, BACK, HID), BF16),
-        in_specs=vmem(7),
-        out_specs=vmem(1)[0],
+        out_shape=(
+            jax.ShapeDtypeStruct((COLS, CAP, HID), BF16),
+            jax.ShapeDtypeStruct((COLS, 1, HID), F32),
+        ),
+        in_specs=hbm(7),
+        out_specs=tuple(vmem(2)),
         scratch_shapes=[
+            pltpu.VMEM(got.shape, BF16),
+            pltpu.VMEM(table.shape, BF16),
+            pltpu.VMEM((CH, HID), BF16),
+            pltpu.VMEM((HID, CH), BF16),
+            pltpu.VMEM((HID, HID), BF16),
+            pltpu.VMEM((HID, HID), BF16),
+            pltpu.VMEM((HID, HID), BF16),
+            pltpu.VMEM((1, HID), BF16),
+            pltpu.VMEM((16, HID), BF16),
+            pltpu.SemaphoreType.DMA((7,)),
             pltpu.VMEM((SLOTS, 2 * HID), BF16),
             pltpu.VMEM((8, SLOTS), F32),
-            pltpu.VMEM((HID, TILE), F32),
-            pltpu.VMEM((HID // 2, TILE), F32),
-            pltpu.VMEM((2 * LINES, S * TILE), BF16),
-            pltpu.VMEM((CH, S * TILE), BF16),
-            pltpu.VMEM((HID, S * TILE), BF16),
-            pltpu.VMEM((S, TILE), F32),
+            pltpu.VMEM((SPACE, TILE, SLOTS), BF16),
+            pltpu.VMEM((SPACE, HID, TILE), F32),
+            pltpu.VMEM((SPACE, HID // 2, TILE), F32),
+            pltpu.VMEM((BUFFERS, 2 * LINES, S * TILE), BF16),
+            pltpu.VMEM((BUFFERS, CH, S * TILE), BF16),
+            pltpu.VMEM((BUFFERS, HID, S * TILE), BF16),
+            pltpu.VMEM((BUFFERS, S, TILE), F32),
+            pltpu.VMEM((SPACE, HID + 16, TILE), BF16),
             pltpu.VMEM((HID + 16, SLOTS), F32),
         ],
-        compiler_params=pltpu.CompilerParams(vmem_limit_bytes=48 << 20),
+        compiler_params=pltpu.CompilerParams(vmem_limit_bytes=58 << 20),
         name="field",
-    )(got, table, w_in, w_mid, w_last, w_feat, jnp.pad(w_density, ((0, 15), (0, 0))))
+    )(got, table, w_in.T, w_mid, w_last, w_feat, w_density)
 
 
 def on_device(
@@ -431,14 +549,15 @@
     w_feat,
     w_density,
 ):
-    got, place = pl.pallas_call(
+    got, place, table = pl.pallas_call(
         ask_kernel,
         out_shape=(
             jax.ShapeDtypeStruct((COLS, ROWS, HID), BF16),
             jax.ShapeDtypeStruct((2, RAYS), jnp.int32),
+            jax.ShapeDtypeStruct((bricks.shape[1], POS * CH, 2 * LINES), BF16),
         ),
-        in_specs=[pl.BlockSpec(memory_space=pl.ANY)] * 5,
-        out_specs=tuple(vmem(2)),
+        in_specs=hbm(6),
+        out_specs=(hbm(1)[0], vmem(1)[0], hbm(1)[0]),
         scratch_shapes=[
             pltpu.VMEM((COLS, ROWS, HID), BF16),
             pltpu.VMEM((1, RAYS), jnp.int32),
@@ -446,13 +565,16 @@
             pltpu.VMEM((S, RAYS), jnp.int32),
             pltpu.VMEM((HID, RAYS), BF16),
             pltpu.VMEM((S, RAYS), BF16),
-            pltpu.SemaphoreType.DMA((5,)),
+            pltpu.VMEM(bricks.shape[1:], BF16),
+            pltpu.VMEM((bricks.shape[1], POS * CH, 2 * LINES), BF16),
+            pltpu.SemaphoreType.DMA((6,)),
+            pltpu.SemaphoreType.DMA,
             pltpu.SemaphoreType.DMA,
             pltpu.SemaphoreType.DMA,
             pltpu.SemaphoreType.DMA,
         ],
         compiler_params=pltpu.CompilerParams(
-            vmem_limit_bytes=32 << 20, collective_id=0, has_side_effects=True
+            vmem_limit_bytes=58 << 20, collective_id=0, has_side_effects=True
         ),
         name="ask",
     )(
@@ -461,9 +583,9 @@
         sample_base[0],
         corner_weights[0].reshape(HID, RAYS),
         spacing[0],
+        bricks[0],
     )
-    table = make_table(bricks[0])
-    block = run_field(got, table, w_in, w_mid, w_last, w_feat, w_density)
+    colour, depth = run_field(got, table, w_in, w_mid, w_last, w_feat, w_density)
     regions = lax.axis_size("depth")
     rows = HID // regions
     return pl.pallas_call(
@@ -472,14 +594,18 @@
             jax.ShapeDtypeStruct((rows, RAYS), F32),
             jax.ShapeDtypeStruct((1, RAYS), F32),
         ),
-        in_specs=vmem(2),
+        in_specs=hbm(2) + vmem(1),
         out_specs=tuple(vmem(2)),
         scratch_shapes=[
-            pltpu.VMEM((COLS, BACK, HID), BF16),
+            pltpu.VMEM((COLS, CAP, HID), BF16),
+            pltpu.VMEM((COLS, 1, HID), F32),
             pltpu.VMEM((regions, rows, RAYS), BF16),
             pltpu.VMEM((1, RAYS), F32),
             pltpu.VMEM((regions, rows, RAYS), BF16),
             pltpu.VMEM((regions, 1, RAYS), F32),
+            pltpu.SemaphoreType.DMA,
+            pltpu.SemaphoreType.DMA,
+            pltpu.SemaphoreType.DMA,
             pltpu.SemaphoreType.DMA,
             pltpu.SemaphoreType.DMA,
             pltpu.SemaphoreType.DMA,
@@ -489,10 +615,10 @@
             pltpu.SemaphoreType.DMA((regions,)),
         ],
         compiler_params=pltpu.CompilerParams(
-            vmem_limit_bytes=32 << 20, collective_id=1, has_side_effects=True
+            vmem_limit_bytes=58 << 20, collective_id=1, has_side_effects=True
         ),
         name="collect",
-    )(block, place)
+    )(colour, depth, place)
 
 
 def solution(mesh):

time: 126 us -> 109 us (0.87)
  Pallas kernels: 121 us -> 105 us
    pallas_call x1, Pallas kernels: 64.6 us -> 46.9 us  [on_device(): pl.pallas_call(collect_kernel, out_shape=(jax.ShapeDtypeStruct((rows, RAY...]
    unnamed x24 -> x2, local copies, waits for them, and re-layouts: 3.58 us -> 2.84 us
where the time goes in v3:
time: 109 us
  Pallas kernels  105 us (96%)
  local copies, waits for them, and re-layouts  2.84 us (3%)
    pallas_call x1, Pallas kernels, on_device(): pl.pallas_call(collect_kernel, out_shape=(jax.ShapeDtypeStruct((rows, RAY...  46.9 us
    pallas_call x1, Pallas kernels, on_device(): pl.pallas_call(ask_kernel, out_shape=(jax.ShapeDtypeStruct((COLS, ROWS, H...  30.5 us
    pallas_call x1, Pallas kernels, run_field(): pl.pallas_call(field_kernel, out_shape=(jax.ShapeDtypeStruct((COLS, CAP,...  27.7 us
    unnamed x2, local copies, waits for them, and re-layouts  2.84 us

profile of v3, /device:TPU:1, one launch (start us, length us, event | category | flops | bytes accessed | tf_op | source)
XLA Modules:
  0.0 108.5 jit_solution(1476195792430911790)
XLA Ops:
  0.6 30.5 %ask.1 = (bf16[64,48,128]{2,1,0:T(8,128)(2,1)}, s32[2,1024]{1,0:T(2,128)}, bf16[4,480,512]{2,1,0:T(8,128)(2,1)}) custom-call(s32[1,1024]{1,0:T(1,128)} %bitcast.11, s32[1,1024]{1,0:T(1,128)} %slot_hbm.1, s32[16,1024]{1,0:T(8,128)} %bitcast.8, bf16[128,1024]{1,0:T(8,128)(2,1)} %bitcast.7, bf16[16,1024]{1,0:T(8,128)(2,1)} %bitcast.9, bf16[4,256,512]{2,1,0:T(8,128)(2,1)} %bitcast.6), custom_call_target="tpu_custom_call" | custom-call | tf_op jit(solution)/shard_map/ask/pallas_call | solution.py:552
  31.2 27.7 %field.1 = (bf16[64,32,128]{2,1,0:T(8,128)(2,1)}, f32[64,1,128]{2,1,0:T(1,128)}) custom-call(bf16[64,48,128]{2,1,0:T(8,128)(2,1)} %get-tuple-element.7.got_hbm, bf16[4,480,512]{2,1,0:T(8,128)(2,1)} %get-tuple-element.8.brick_hbm, bf16[32,128]{1,0:T(8,128)(2,1)} %bitcast.10, bf16[128,128]{1,0:T(8,128)(2,1)} %w_mid_hbm.1, bf16[128,128]{1,0:T(8,128)(2,1)} %w_last_hbm.1, ...), custom_call_target="tpu_custom_call" | custom-call | tf_op jit(solution)/shard_map/field/pallas_call | solution.py:503
  58.8 46.9 %collect.1 = (f32[32,1024]{1,0:T(8,128)}, f32[1,1024]{1,0:T(1,128)}) custom-call(bf16[64,32,128]{2,1,0:T(8,128)(2,1)} %get-tuple-element.9.colour_ref, f32[64,1,128]{2,1,0:T(1,128)} %get-tuple-element.10.depth_ref, s32[2,1024]{1,0:T(2,128)} %get-tuple-element.11.place_ref), custom_call_target="tpu_custom_call" | custom-call | tf_op jit(solution)/shard_map/collect/pallas_call | solution.py:591
  105.7 1.6 %copy.15 = f32[32,1024]{1,0:T(8,128)} copy(f32[32,1024]{1,0:T(8,128)} %get-tuple-element.14) | data formatting | bytes 262144
  107.3 1.3 %copy.16 = f32[1,1024]{1,0:T(1,128)} copy(f32[1,1024]{1,0:T(1,128)} %get-tuple-element.15) | data formatting | bytes 8192

commit v4 on v3

--- a/solution.py
+++ b/solution.py
@@ -304,16 +304,18 @@
         mixed = jnp.zeros((CH, WIDE), F32)
         for p in range(POS):
             mixed = jnp.where(coord_z == float(p), read[p * CH : (p + 1) * CH], mixed)
-        mixed_ref[u, :, lanes] = mixed.astype(BF16)
-
-    def shade(u):
-        layer = mixed_ref[u]
+        mixed_ref[:, slice(u * S * TILE + group * WIDE, u * S * TILE + (group + 1) * WIDE)] = mixed.astype(BF16)
+
+    def shade():
+        layer = mixed_ref[...]
         for w_ref in (w_in_ref, w_mid_ref, w_last_ref):
             layer = jnp.maximum(dot(w_ref[...], layer), 0.0).astype(BF16)
-        hidden_ref[u] = layer
+        hidden_ref[...] = layer
         thin = dot(w_density_ref[...], layer)
-        for s in range(S):
-            density_ref[u, s : s + 1, :] = thin[0:1, s * TILE : (s + 1) * TILE]
+        for u in range(BUFFERS):
+            for s in range(S):
+                start = (u * S + s) * TILE
+                density_ref[u, s : s + 1, :] = thin[0:1, start : start + TILE]
 
     def composite(tile, u):
         density = density_ref[u]
@@ -326,7 +328,8 @@
         share = clear * (1.0 - jnp.exp(-optical))
         total = jnp.zeros((HID, TILE), F32)
         for s in range(S):
-            hidden = hidden_ref[u, :, s * TILE : (s + 1) * TILE].astype(F32)
+            start = (u * S + s) * TILE
+            hidden = hidden_ref[:, start : start + TILE].astype(F32)
             total = total + hidden * share[s : s + 1]
         high = total.astype(BF16)
         low = (total - high.astype(F32)).astype(BF16)
@@ -355,14 +358,12 @@
             spread(tile, 0, group)
             for s in range(EACH):
                 build(tile + 1, 1, group * EACH + s)
-        shade(0)
         for group in range(groups):
             spread(tile + 1, 1, group)
             for s in range(EACH):
                 build(following, 0, group * EACH + s)
-            if group == groups // 2:
-                composite(tile, 0)
-        shade(1)
+        shade()
+        composite(tile, 0)
         composite(tile + 1, 1)
         return carried
 
@@ -525,8 +526,8 @@
             pltpu.VMEM((SPACE, HID, TILE), F32),
             pltpu.VMEM((SPACE, HID // 2, TILE), F32),
             pltpu.VMEM((BUFFERS, 2 * LINES, S * TILE), BF16),
-            pltpu.VMEM((BUFFERS, CH, S * TILE), BF16),
-            pltpu.VMEM((BUFFERS, HID, S * TILE), BF16),
+            pltpu.VMEM((CH, BUFFERS * S * TILE), BF16),
+            pltpu.VMEM((HID, BUFFERS * S * TILE), BF16),
             pltpu.VMEM((BUFFERS, S, TILE), F32),
             pltpu.VMEM((SPACE, HID + 16, TILE), BF16),
             pltpu.VMEM((HID + 16, SLOTS), F32),
@@ -615,7 +616,7 @@
             pltpu.SemaphoreType.DMA((regions,)),
         ],
         compiler_params=pltpu.CompilerParams(
-            vmem_limit_bytes=58 << 20, collective_id=1, has_side_effects=True
+            vmem_limit_bytes=56098816, collective_id=1, has_side_effects=True
         ),
         name="collect",
     )(colour, depth, place)

time: 109 us -> 108 us (level)
    pallas_call x1, Pallas kernels: 27.7 us -> 21.4 us  [run_field(): pl.pallas_call(field_kernel, out_shape=(jax.ShapeDtypeStruct((COLS, CAP,...]
    pallas_call x1, Pallas kernels: 46.9 us -> 52.7 us  [on_device(): pl.pallas_call(collect_kernel, out_shape=(jax.ShapeDtypeStruct((rows, RAY...]
    unnamed x2 -> x6, local copies, waits for them, and re-layouts: 2.84 us -> 2.01 us
where the time goes in v4:
time: 108 us; the launch traced here: 107 us
  Pallas kernels  105 us (97%)
  local copies, waits for them, and re-layouts  2.01 us (2%)
    pallas_call x1, Pallas kernels, on_device(): pl.pallas_call(collect_kernel, out_shape=(jax.ShapeDtypeStruct((rows, RAY...  52.7 us
    pallas_call x1, Pallas kernels, on_device(): pl.pallas_call(ask_kernel, out_shape=(jax.ShapeDtypeStruct((COLS, ROWS, H...  30.5 us
    pallas_call x1, Pallas kernels, run_field(): pl.pallas_call(field_kernel, out_shape=(jax.ShapeDtypeStruct((COLS, CAP,...  21.4 us

profile of v4, /device:TPU:1, one launch (start us, length us, event | category | flops | bytes accessed | tf_op | source)
XLA Modules:
  0.0 107.3 jit_solution(6447967307481861813)
XLA Ops:
  0.6 30.5 %ask.1 = (bf16[64,48,128]{2,1,0:T(8,128)(2,1)}, s32[2,1024]{1,0:T(2,128)}, bf16[4,480,512]{2,1,0:T(8,128)(2,1)}) custom-call(s32[1,1024]{1,0:T(1,128)} %bitcast.11, s32[1,1024]{1,0:T(1,128)} %slot_hbm.1, s32[16,1024]{1,0:T(8,128)} %bitcast.8, bf16[128,1024]{1,0:T(8,128)(2,1)} %bitcast.7, bf16[16,1024]{1,0:T(8,128)(2,1)} %bitcast.9, bf16[4,256,512]{2,1,0:T(8,128)(2,1)} %bitcast.6), custom_call_target="tpu_custom_call" | custom-call | tf_op jit(solution)/shard_map/ask/pallas_call | solution.py:553
  31.2 0.0 copy-start.1
  31.2 21.4 %field.1 = (bf16[64,32,128]{2,1,0:T(8,128)(2,1)}, f32[64,1,128]{2,1,0:T(1,128)}) custom-call(bf16[64,48,128]{2,1,0:T(8,128)(2,1)} %get-tuple-element.7.got_hbm, bf16[4,480,512]{2,1,0:T(8,128)(2,1)} %get-tuple-element.8.brick_hbm, bf16[32,128]{1,0:T(8,128)(2,1)} %bitcast.10, bf16[128,128]{1,0:T(8,128)(2,1)} %w_mid_hbm.1, bf16[128,128]{1,0:T(8,128)(2,1)} %w_last_hbm.1, ...), custom_call_target="tpu_custom_call" | custom-call | tf_op jit(solution)/shard_map/field/pallas_call | solution.py:504
  52.6 0.0 copy-done.1
  52.6 0.0 copy-start
  52.6 0.7 copy-done
  53.3 52.7 %collect.1 = (f32[32,1024]{1,0:T(8,128)S(1)}, f32[1,1024]{1,0:T(1,128)S(1)}) custom-call(bf16[64,32,128]{2,1,0:T(8,128)(2,1)} %get-tuple-element.9.colour_ref, f32[64,1,128]{2,1,0:T(1,128)S(1)} %copy-done, s32[2,1024]{1,0:T(2,128)S(1)} %copy-done.1), custom_call_target="tpu_custom_call" | custom-call | tf_op jit(solution)/shard_map/collect/pallas_call | solution.py:592
  106.1 0.7 copy.15
  106.7 0.6 copy.16
Async XLA Ops:
  31.2 21.4 %copy-start.1 = (s32[2,1024]{1,0:T(2,128)S(1)}, s32[2,1024]{1,0:T(2,128)}, u32[]{:S(2)}) copy-start(s32[2,1024]{1,0:T(2,128)} %get-tuple-element.11.place_ref) | copy-start | bytes 24580
  52.6 0.8 copy-start
